TPU v7x, 256 devices: a whole 4x4x8 slice. The times are simulated.
256 devices in a mesh: seq: 32 (over x, y, core), ch: 8 (over z).
Axes of the slice: x: 4, y: 4, z: 8, core: 2. Of those that a mesh axis runs over, the one named last changes fastest.
Arguments:
- inputs: bfloat16 [256, 131072], P('ch', 'seq'), may hold values from -6 to 6
- w_in: bfloat16 [3, 256, 256], P(None, 'ch'), may hold values from -0.375 to 0.375
- b_in: float32 [3, 256], P(None, 'ch'), may hold values from -3 to 3
- short_kernel: float32 [3, 256, 3], P(None, 'ch'), may hold values from -1 to 1
- positional: float32 [5, 131072], P(None, 'seq'), may hold values from -3.5 to 3.5
- filter_in: float32 [64, 5], replicated, may hold values from -4 to 4
- filter_bias: float32 [3, 64], replicated, may hold values from -4 to 4
- filter_freq: float32 [3, 64], replicated, may hold values from 0.5 to 2
- filter_hidden: float32 [2, 64, 64], replicated, may hold values from -0.75 to 0.75
- filter_out: float32 [256, 64], P('ch'), may hold values from -0.01171875 to 0.01171875
- decay: float32 [256], P('ch'), may hold values from 0.05 to 8
- conv_bias: float32 [256], P('ch'), may hold values from -1.5 to 1.5
- w_out: bfloat16 [256, 256], replicated, may hold values from -0.375 to 0.375
- b_out: float32 [256], P('ch'), may hold values from -3 to 3
Outputs:
- outputs: bfloat16 [256, 131072], P('ch', 'seq')
All inputs are finite; a program needn't handle non-finite values.
Results may differ from a plain program's by a relative error of at most 0.005.
Values may be sent and summed in bfloat16 or wider, within the bound.
A program may use at most 64 MiB of HBM per device.

v0:
```python
import math

import jax
import jax.numpy as jnp
import numpy as np
from jax import lax
from jax.experimental import pallas as pl
from jax.experimental.pallas import tpu as pltpu
from jax.sharding import PartitionSpec as P

MESH = pl.DeviceIdType.MESH
F32 = jnp.float32
BF16 = jnp.bfloat16
HIGHEST = lax.Precision.HIGHEST

SEQ, CH = 32, 8
DEV = SEQ * CH
D = 256
OWN = D // CH
SPAN = 4096
CHUNK = SPAN // CH
LENGTH = SPAN * SEQ
HALO = 128
LANES = 128
RADIX = CHUNK // LANES
ORDER = 64
BIAS, TAPS, DECAY, DIRECT, OUTB = 64, 67, 76, 77, 78


def halves(table):
    high = np.asarray(table, np.float64).astype(jnp.bfloat16)
    low = (np.asarray(table, np.float64) - high.astype(np.float64)).astype(jnp.bfloat16)
    return high, low


def tables():
    rows = np.arange(D)
    f1 = np.arange(D) + 0.25
    angle = 2.0 * np.pi * ((np.outer(4 * f1, rows) % (4 * D)) / (4 * D))
    first = np.concatenate([np.cos(angle), -np.sin(angle)], axis=0)
    first_stack = np.concatenate(halves(first), axis=0)
    last_stack = np.concatenate(halves(first.T / LENGTH), axis=0)
    lanes = np.arange(LANES)
    inner = 2.0 * np.pi * (np.outer(lanes, lanes) % LANES) / LANES
    c, s = np.cos(inner), np.sin(inner)
    forward = np.stack(halves(np.block([[c, -s], [s, c]])))
    inverse = np.stack(halves(np.block([[c, s], [-s, c]])))
    shift = f1[:, None] + D * np.arange(RADIX)[None, :]
    turn = 2.0 * np.pi / LENGTH * shift[:, :, None] * lanes[None, None, :]
    turn = turn.reshape(D, CHUNK)
    twiddle = np.stack([np.cos(turn), np.sin(turn)]).astype(np.float32)
    spin = 2.0 * np.pi / (RADIX * D) * f1[:, None] * np.arange(RADIX)[None, :]
    spins = np.zeros((D, LANES), np.float32)
    spins[:, 0:RADIX] = np.cos(spin)
    spins[:, RADIX : 2 * RADIX] = np.sin(spin)
    return first_stack, last_stack, forward, inverse, twiddle, spins


def split(x):
    high = x.astype(BF16)
    return high, (x - high.astype(F32)).astype(BF16)


def mm(a, b):
    return jnp.dot(a, b, preferred_element_type=F32)


def kernel(
    x_ref,
    w_ref,
    prm_ref,
    pos_ref,
    net_ref,
    hid_ref,
    wout_ref,
    first_ref,
    last_ref,
    fwd_ref,
    inv_ref,
    twid_ref,
    spin_ref,
    out_ref,
    xc,
    wbuf,
    pbuf,
    proj,
    stage,
    keep0,
    keepg,
    snd,
    rcv,
    first_v,
    last_v,
    fwd_v,
    inv_v,
    twid_v,
    spin_v,
    sect,
    chi,
    clo,
    back,
    dhi,
    dlo,
    ystage,
    ysnd,
    yrcv,
    osnd,
    const_sem,
    s1,
    rx,
    rh,
    rw,
    rp,
    s3,
    r3,
    s5,
    r5,
    s6,
    r6,
    ):
    s = lax.axis_index("seq")
    c = lax.axis_index("ch")
    me = s * CH + c
    own = pl.multiple_of(c * OWN, OWN)
    rows_own = pl.ds(own, OWN)

    consts = [
        pltpu.make_async_copy(src, dst, const_sem.at[i])
        for i, (src, dst) in enumerate(
            [
                (first_ref, first_v),
                (last_ref, last_v),
                (fwd_ref, fwd_v),
                (inv_ref, inv_v),
                (twid_ref, twid_v),
                (spin_ref, spin_v),
            ]
        )
    ]

    def put(src, dst, send, recv, to):
        pltpu.make_async_remote_copy(
            src_ref=src, dst_ref=dst, send_sem=send, recv_sem=recv, device_id=to, device_id_type=MESH
        ).start()

    x_dst = xc.at[rows_own, pl.ds(HALO, CHUNK)]
    h_dst = xc.at[rows_own, pl.ds(0, HALO)]
    w_dst = wbuf.at[:, rows_own, :]
    p_dst = pbuf.at[rows_own, :]
    for i in range(1, CH):
        j = lax.rem(c + i, CH)
        put(prm_ref, p_dst, s1.at[3], rp, (s, j))
    for i in range(1, CH):
        j = lax.rem(c + i, CH)
        put(
            x_ref.at[:, pl.ds(pl.multiple_of(j * CHUNK, CHUNK), CHUNK)], x_dst, s1.at[0], rx, (s, j)
        )
        put(w_ref, w_dst, s1.at[2], rw, (s, j))

    def tail(j):
        return x_ref.at[:, pl.ds(pl.multiple_of(j * CHUNK + CHUNK - HALO, HALO), HALO)]

    for i in range(1, CH):
        j = lax.rem(c + i, CH)

        @pl.when(j > 0)
        def _():
            put(tail(j - 1), h_dst, s1.at[1], rh, (s, j))

    @pl.when(s < SEQ - 1)
    def _():
        put(tail(CH - 1), h_dst, s1.at[1], rh, (s + 1, 0))

    pltpu.make_async_copy(
        x_ref.at[:, pl.ds(pl.multiple_of(c * CHUNK, CHUNK), CHUNK)], x_dst, rx
    ).start()
    pltpu.make_async_copy(w_ref, w_dst, rw).start()
    pltpu.make_async_copy(prm_ref, p_dst, rp).start()

    @pl.when(c > 0)
    def _():
        pltpu.make_async_copy(tail(c - 1), h_dst, rh).start()

    @pl.when(me == 0)
    def _():
        xc[:, 0:HALO] = jnp.zeros((D, HALO), BF16)

    for copy in consts:
        copy.start()

    here = pl.ds(pl.multiple_of(c * CHUNK, CHUNK), CHUNK)
    net = net_ref[...]
    inner = net[:, 0:1] * pos_ref[0:1, here]
    for i in range(1, 5):
        inner = inner + net[:, i : i + 1] * pos_ref[i : i + 1, here]
    activity = jnp.sin(net[:, 8:9] * (inner + net[:, 5:6]))
    for layer in range(2):
        inner = (
            jnp.dot(hid_ref[layer], activity, precision=HIGHEST, preferred_element_type=F32)
            + net[:, 6 + layer : 7 + layer]
        )
        activity = jnp.sin(net[:, 9 + layer : 10 + layer] * inner)
    places = me * CHUNK + lax.broadcasted_iota(jnp.int32, (1, CHUNK), 1)
    scaled = places.astype(F32) / (LENGTH - 1)

    def wait(ref, sem):
        pltpu.make_async_copy(ref, ref, sem).wait()

    wait(pbuf, rp)
    for lo in range(0, D, 64):
        pm = pbuf[lo : lo + 64, :]
        values = jnp.dot(pm[:, 0:ORDER], activity, precision=HIGHEST, preferred_element_type=F32)
        values = values * jnp.exp(-(scaled * pm[:, DECAY : DECAY + 1]))
        for r in range(RADIX):
            stage[pl.ds(8 * lo + RADIX + r, 64, stride=8), :] = values[
                :, r * LANES : (r + 1) * LANES
            ]

    wait(xc.at[:, pl.ds(HALO, CHUNK)], rx)
    wait(wbuf, rw)

    @pl.when(me > 0)
    def _():
        wait(xc.at[:, pl.ds(0, HALO)], rh)

    for j in range(3):
        proj[j] = mm(wbuf[j], xc[...])
    column = lax.broadcasted_iota(jnp.int32, (1, HALO + CHUNK), 1)
    inside = jnp.logical_or(column >= HALO, me > 0)

    def shorts(step, carry):
        lo = pl.multiple_of(step * 32, 32)
        pm = pbuf[pl.ds(lo, 32), :]
        streams = []
        for j in range(3):
            p = jnp.where(inside, proj[j, pl.ds(lo, 32), :] + pm[:, BIAS + j : BIAS + j + 1], 0.0)
            taps = [pm[:, TAPS + 3 * j + i : TAPS + 3 * j + i + 1] for i in range(3)]
            streams.append(
                taps[0] * pltpu.roll(p, 2, 1)[:, HALO:]
                + taps[1] * pltpu.roll(p, 1, 1)[:, HALO:]
                + taps[2] * p[:, HALO:]
            )
        gated = streams[2] * streams[1]
        keep0[pl.ds(lo, 32), :] = streams[0]
        keepg[pl.ds(lo, 32), :] = gated
        for r in range(RADIX):
            stage[pl.ds(8 * lo + r, 32, stride=8), :] = gated[:, r * LANES : (r + 1) * LANES]
        return carry

    lax.fori_loop(0, D // 32, shorts, 0)
    snd[...] = stage[...].reshape(D, 8, LANES).astype(BF16)

    def scatter(src, dst, send, recv):
        def one(i, carry):
            to = lax.rem(me + i, DEV)
            put(src.at[to], dst.at[me], send, recv, (to // CH, lax.rem(to, CH)))
            return carry

        lax.fori_loop(1, DEV, one, 0)
        pltpu.make_async_copy(src.at[me], dst.at[me], recv).start()

    scatter(snd, rcv, s3, r3)
    for copy in consts:
        copy.wait()
    wait(rcv, r3)

    stage[...] = rcv[...].astype(F32).reshape(D * 8, LANES)
    for r in range(RADIX):
        x = jnp.concatenate(
            [stage[pl.ds(r, D, stride=8), :], stage[pl.ds(RADIX + r, D, stride=8), :]], axis=1
        ).astype(BF16)
        for part in range(2):
            sect[r, part] = mm(first_v[part * D : (part + 1) * D, :], x) + mm(
                first_v[(2 + part) * D : (3 + part) * D, :], x
            )

    def ahead(step, carry):
        lo = pl.multiple_of(step * 16, 16)
        rows = pl.ds(lo, 16)
        spins = spin_v[rows, :]
        re, im = [], []
        for r in range(RADIX):
            a, b = sect[r, 0, rows, :], sect[r, 1, rows, :]
            if r:
                cs, sn = spins[:, r : r + 1], spins[:, RADIX + r : RADIX + r + 1]
                a, b = a * cs + b * sn, b * cs - a * sn
            re.append(a)
            im.append(b)
        e0r, e0i, e1r, e1i = re[0] + re[2], im[0] + im[2], re[0] - re[2], im[0] - im[2]
        o0r, o0i, o1r, o1i = re[1] + re[3], im[1] + im[3], re[1] - re[3], im[1] - im[3]
        outs = [
            (e0r + o0r, e0i + o0i),
            (e1r + o1i, e1i - o1r),
            (e0r - o0r, e0i - o0i),
            (e1r - o1i, e1i + o1r),
        ]
        for h, (a, b) in enumerate(outs):
            cs = twid_v[0, rows, h * LANES : (h + 1) * LANES]
            sn = twid_v[1, rows, h * LANES : (h + 1) * LANES]
            for g in range(2):
                ga = a[:, g * LANES : (g + 1) * LANES]
                gb = b[:, g * LANES : (g + 1) * LANES]
                pair = jnp.concatenate([ga * cs + gb * sn, gb * cs - ga * sn], axis=1)
                high, low = split(pair)
                chi[g, h, rows, :] = high
                clo[g, h, rows, :] = low
        return carry

    lax.fori_loop(0, D // 16, ahead, 0)

    for h in range(RADIX):
        spectra = []
        for g in range(2):
            high, low = chi[g, h], clo[g, h]
            spectra.append(mm(high, fwd_v[0]) + mm(low, fwd_v[0]) + mm(high, fwd_v[1]))
        (gr, gi), (kr, ki) = [(z[:, :LANES], z[:, LANES:]) for z in spectra]
        product = jnp.concatenate([gr * kr - gi * ki, gr * ki + gi * kr], axis=1)
        high, low = split(product)
        z = mm(high, inv_v[0]) + mm(low, inv_v[0]) + mm(high, inv_v[1])
        zr, zi = z[:, :LANES], z[:, LANES:]
        cs = twid_v[0, :, h * LANES : (h + 1) * LANES]
        sn = twid_v[1, :, h * LANES : (h + 1) * LANES]
        back[h, 0] = zr * cs - zi * sn
        back[h, 1] = zi * cs + zr * sn

    def behind(step, carry):
        lo = pl.multiple_of(step * 16, 16)
        rows = pl.ds(lo, 16)
        rows_im = pl.ds(pl.multiple_of(D + lo, 16), 16)
        spins = spin_v[rows, :]
        re = [back[h, 0, rows, :] for h in range(RADIX)]
        im = [back[h, 1, rows, :] for h in range(RADIX)]
        e0r, e0i, e1r, e1i = re[0] + re[2], im[0] + im[2], re[0] - re[2], im[0] - im[2]
        o0r, o0i, o1r, o1i = re[1] + re[3], im[1] + im[3], re[1] - re[3], im[1] - im[3]
        outs = [
            (e0r + o0r, e0i + o0i),
            (e1r - o1i, e1i + o1r),
            (e0r - o0r, e0i - o0i),
            (e1r + o1i, e1i - o1r),
        ]
        for r, (a, b) in enumerate(outs):
            if r:
                cs, sn = spins[:, r : r + 1], spins[:, RADIX + r : RADIX + r + 1]
                a, b = a * cs - b * sn, b * cs + a * sn
            lanes = slice(r * LANES, (r + 1) * LANES)
            high, low = split(a)
            dhi[rows, lanes] = high
            dlo[rows, lanes] = low
            high, low = split(b)
            dhi[rows_im, lanes] = high
            dlo[rows_im, lanes] = low
        return carry

    lax.fori_loop(0, D // 16, behind, 0)
    last_hi, last_lo = last_v[0:D, :], last_v[D : 2 * D, :]
    settled = mm(last_hi, dhi[...]) + mm(last_lo, dhi[...]) + mm(last_hi, dlo[...])
    for r in range(RADIX):
        ystage[:, r, :] = settled[:, r * LANES : (r + 1) * LANES]
    ysnd[...] = ystage[...].astype(BF16)

    scatter(ysnd, yrcv, s5, r5)
    wait(yrcv, r5)

    ystage[...] = yrcv[...].astype(F32)
    convolved = jnp.concatenate([ystage[:, r, :] for r in range(RADIX)], axis=1)
    convolved = convolved + pbuf[:, DIRECT : DIRECT + 1] * keepg[...]
    mixed = (keep0[...] * convolved).astype(BF16)
    osnd[...] = (mm(wout_ref[...], mixed) + pbuf[:, OUTB : OUTB + 1]).astype(BF16)
    o_dst = out_ref.at[:, pl.ds(pl.multiple_of(c * CHUNK, CHUNK), CHUNK)]
    for i in range(1, CH):
        j = lax.rem(c + i, CH)
        put(osnd.at[pl.ds(pl.multiple_of(j * OWN, OWN), OWN), :], o_dst, s6, r6, (s, j))
    pltpu.make_async_copy(osnd.at[rows_own, :], o_dst, r6).start()

    wait(out_ref, r6)
    rest = pl.ds(0, D - OWN)
    wait(xc.at[rest, pl.ds(HALO, CHUNK)], s1.at[0])
    wait(wbuf.at[:, rest, :], s1.at[2])
    wait(pbuf.at[rest, :], s1.at[3])
    six = pl.ds(0, 6 * OWN)
    wait(xc.at[six, pl.ds(0, HALO)], s1.at[1])

    @pl.when(c == 0)
    def _():
        wait(xc.at[pl.ds(0, OWN), pl.ds(0, HALO)], s1.at[1])

    @pl.when(s < SEQ - 1)
    def _():
        wait(xc.at[pl.ds(0, OWN), pl.ds(0, HALO)], s1.at[1])

    wait(snd.at[pl.ds(0, DEV - 1)], s3)
    wait(ysnd.at[pl.ds(0, DEV - 1)], s5)
    wait(osnd.at[rest, :], s6)


def body(
    inputs,
    w_in,
    b_in,
    short_kernel,
    positional,
    filter_in,
    filter_bias,
    filter_freq,
    filter_hidden,
    filter_out,
    decay,
    conv_bias,
    w_out,
    b_out,
):
    prm = jnp.concatenate(
        [
            filter_out,
            b_in.T,
            short_kernel.transpose(1, 0, 2).reshape(OWN, 9),
            decay[:, None],
            conv_bias[:, None],
            b_out[:, None],
            jnp.zeros((OWN, LANES - 79), F32),
        ],
        axis=1,
    )
    net = jnp.concatenate(
        [filter_in, filter_bias.T, filter_freq.T, jnp.zeros((ORDER, LANES - 11), F32)], axis=1
    )
    hbm = pl.BlockSpec(memory_space=pl.ANY)
    vmem = pl.BlockSpec(memory_space=pltpu.VMEM)
    dma = pltpu.SemaphoreType.DMA
    return pl.pallas_call(
        kernel,
        out_shape=jax.ShapeDtypeStruct((OWN, SPAN), BF16),
        in_specs=[hbm, hbm, hbm, vmem, vmem, vmem, vmem] + [hbm] * 6,
        out_specs=vmem,
        scratch_shapes=[
            pltpu.VMEM((D, HALO + CHUNK), BF16),
            pltpu.VMEM((3, D, D), BF16),
            pltpu.VMEM((D, LANES), F32),
            pltpu.VMEM((3, D, HALO + CHUNK), F32),
            pltpu.VMEM((D * 8, LANES), F32),
            pltpu.VMEM((D, CHUNK), F32),
            pltpu.VMEM((D, CHUNK), F32),
            pltpu.VMEM((DEV, 8, LANES), BF16),
            pltpu.VMEM((DEV, 8, LANES), BF16),
            pltpu.VMEM((4 * D, D), BF16),
            pltpu.VMEM((2 * D, 2 * D), BF16),
            pltpu.VMEM((2, D, D), BF16),
            pltpu.VMEM((2, D, D), BF16),
            pltpu.VMEM((2, D, CHUNK), F32),
            pltpu.VMEM((D, LANES), F32),
            pltpu.VMEM((RADIX, 2, D, 2 * LANES), F32),
            pltpu.VMEM((2, RADIX, D, 2 * LANES), BF16),
            pltpu.VMEM((2, RADIX, D, 2 * LANES), BF16),
            pltpu.VMEM((RADIX, 2, D, LANES), F32),
            pltpu.VMEM((2 * D, CHUNK), BF16),
            pltpu.VMEM((2 * D, CHUNK), BF16),
            pltpu.VMEM((DEV, RADIX, LANES), F32),
            pltpu.VMEM((DEV, RADIX, LANES), BF16),
            pltpu.VMEM((DEV, RADIX, LANES), BF16),
            pltpu.VMEM((D, CHUNK), BF16),
            dma((6,)),
            dma((4,)),
            dma,
            dma,
            dma,
            dma,
            dma,
            dma,
            dma,
            dma,
            dma,
            dma,
        ],
        compiler_params=pltpu.CompilerParams(has_side_effects=True),
    )(inputs, w_in, prm, positional, net, filter_hidden, w_out, *tables())


def solution(mesh):
    in_specs = (
        P("ch", "seq"),
        P(None, "ch", None),
        P(None, "ch"),
        P(None, "ch", None),
        P(None, "seq"),
        P(),
        P(),
        P(),
        P(),
        P("ch", None),
        P("ch"),
        P("ch"),
        P(),
        P("ch"),
    )
    return jax.shard_map(
        body, mesh=mesh, in_specs=in_specs, out_specs=P("ch", "seq"), check_vma=False
    )
```

profile of v0, /device:TPU:1, one launch (start us, length us, event | category | flops | bytes accessed | tf_op | source)
XLA Modules:
  0.0 96.4 jit_solution(18418703965827768981)
XLA Ops:
  0.0 0.0 copy-start.1
  0.0 0.1 pad.3.clone
  0.1 0.6 copy-done.1
  0.7 0.0 copy-start.3
  0.7 0.1 copy.30
  0.8 0.6 copy-done.3
  1.4 0.1 copy.29
  1.5 0.0 copy-start.6
  1.5 0.7 copy-done.6
  2.1 0.0 copy-start.7
  2.1 0.1 copy.31
  2.2 0.6 copy-done.7
  2.8 0.0 copy-start.8
  2.8 0.1 copy.32
  2.9 0.6 copy-done.8
  3.4 0.0 copy-start
  3.4 0.1 copy.33
  3.5 0.6 copy-done
  4.2 0.0 copy-start.2
  4.2 0.7 concatenate.6.prm_ref
  4.8 0.0 copy-done.2
  4.8 0.0 copy-start.4
  4.9 0.1 copy.36
  4.9 0.6 copy-done.4
  5.5 0.0 copy-start.5
  5.5 0.1 copy.34
  5.6 0.6 copy-done.5
  6.2 0.1 copy.35
  6.3 0.7 maximum_maximum_fusion.net_ref
  7.0 87.7 %shard_map.190 = bf16[32,4096]{1,0:T(8,128)(2,1)} custom-call(bf16[32,4096]{1,0:T(8,128)(2,1)} %x_ref.1, bf16[3,32,256]{2,1,0:T(8,128)(2,1)} %w_ref.1, f32[32,128]{1,0:T(8,128)} %concatenate.6.prm_ref, f32[5,4096]{1,0:T(8,128)} %pos_ref.1, f32[64,128]{1,0:T(8,128)} %maximum_maximum_fusion.net_ref, f32[2,64,64]{2,1,0:T(8,128)} %hid_ref.1, ...), custom_call_target="tpu_custom_call" | custom-call | tf_op jit(solution)/shard_map/pallas_call | solution.py:430
  94.7 1.7 %copy.38 = bf16[32,4096]{1,0:T(8,128)(2,1)} copy(bf16[32,4096]{1,0:T(8,128)(2,1)} %shard_map.190) | data formatting | bytes 524288
  (3 shorter events, 0.0 us)
Async XLA Ops:
  0.0 0.7 copy-start.1
  0.7 0.7 copy-start.3
  1.5 0.7 copy-start.6
  2.1 0.7 copy-start.7
  2.8 0.7 copy-start.8
  3.4 0.7 copy-start
  4.2 0.7 copy-start.2
  4.8 0.7 copy-start.4
  5.5 0.7 copy-start.5
where the time goes:
time: 96.7 us; the launch traced here: 96.4 us
  Pallas kernels  87.7 us (91%)
  local copies, waits for them, and re-layouts  7.96 us (8%)
    pallas_call x1, Pallas kernels, body(): pl.pallas_call(kernel, out_shape=jax.ShapeDtypeStruct((OWN, SPAN), BF16),...  87.7 us
    unnamed x23, local copies, waits for them, and re-layouts  6.84 us

commit v1 on v0

v1 whole, which is shorter than its diff:
```python
import math

import jax
import jax.numpy as jnp
import numpy as np
from jax import lax
from jax.experimental import pallas as pl
from jax.experimental.pallas import tpu as pltpu
from jax.sharding import PartitionSpec as P

MESH = pl.DeviceIdType.MESH
F32 = jnp.float32
BF16 = jnp.bfloat16
HIGHEST = lax.Precision.HIGHEST

SEQ, CH = 32, 8
DEV = SEQ * CH
D = 256
OWN = D // CH
SPAN = 4096
CHUNK = SPAN // CH
LENGTH = SPAN * SEQ
HALO = 128
LANES = 128
RADIX = CHUNK // LANES
ORDER = 64
BLOCK = 16
BIAS, TAPS, DECAY, DIRECT, OUTB = 64, 67, 76, 77, 78


def halves(table):
    high = np.asarray(table, np.float64).astype(jnp.bfloat16)
    low = (np.asarray(table, np.float64) - high.astype(np.float64)).astype(jnp.bfloat16)
    return high, low


def tables():
    rows = np.arange(D)
    f1 = np.arange(D) + 0.25
    angle = 2.0 * np.pi * ((np.outer(4 * f1, rows) % (4 * D)) / (4 * D))
    first = np.concatenate([np.cos(angle), -np.sin(angle)], axis=0)
    first_stack = np.concatenate(halves(first), axis=0)
    last_stack = np.concatenate(halves(first.T / LENGTH), axis=0)
    lanes = np.arange(LANES)
    inner = 2.0 * np.pi * (np.outer(lanes, lanes) % LANES) / LANES
    c, s = np.cos(inner), np.sin(inner)
    forward = np.stack(halves(np.block([[c, -s], [s, c]])))
    inverse = np.stack(halves(np.block([[c, s], [-s, c]])))
    shift = f1[:, None] + D * np.arange(RADIX)[None, :]
    turn = 2.0 * np.pi / LENGTH * shift[:, :, None] * lanes[None, None, :]
    turn = turn.reshape(D, CHUNK)
    twiddle = np.stack([np.cos(turn), np.sin(turn)]).astype(np.float32)
    spin = 2.0 * np.pi / (RADIX * D) * f1[:, None] * np.arange(RADIX)[None, :]
    spins = np.zeros((D, LANES), np.float32)
    spins[:, 0:RADIX] = np.cos(spin)
    spins[:, RADIX : 2 * RADIX] = np.sin(spin)
    return first_stack, last_stack, forward, inverse, twiddle, spins


def split(x):
    high = x.astype(BF16)
    return high, (x - high.astype(F32)).astype(BF16)


def mm(a, b):
    return jnp.dot(a, b, preferred_element_type=F32)


def kernel(
    x_ref,
    w_ref,
    bin_ref,
    taps_ref,
    fout_ref,
    decay_ref,
    direct_ref,
    bout_ref,
    pos_ref,
    fin_ref,
    fbias_ref,
    ffreq_ref,
    fhid_ref,
    wout_ref,
    first_ref,
    last_ref,
    fwd_ref,
    inv_ref,
    twid_ref,
    spin_ref,
    out_ref,
    bin_v,
    taps_v,
    fout_v,
    decay_v,
    direct_v,
    bout_v,
    pos_v,
    fin_v,
    fbias_v,
    ffreq_v,
    fhid_v,
    wout_v,
    raw,
    rawnet,
    prm,
    xc,
    wbuf,
    pbuf,
    pflat,
    proj,
    stage,
    keep0,
    keepg,
    ksnd,
    krcv,
    gsnd,
    grcv,
    first_v,
    last_v,
    fwd_v,
    inv_v,
    twid_v,
    spin_v,
    sect,
    chi,
    clo,
    spec,
    back,
    dhi,
    dlo,
    ysnd,
    yrcv,
    osnd,
    small_sem,
    const_sem,
    gate,
    s1,
    r1,
    s3,
    r3,
    s6,
    r6,
):
    s = lax.axis_index("seq")
    c = lax.axis_index("ch")
    me = s * CH + c
    y = lax.rem(s // 2, 4)
    own = pl.multiple_of(c * OWN, OWN)
    rows_own = pl.ds(own, OWN)

    smalls = [
        pltpu.make_async_copy(src, dst, small_sem.at[i])
        for i, (src, dst) in enumerate(
            [
                (bin_ref, bin_v),
                (taps_ref, taps_v),
                (fout_ref, fout_v),
                (decay_ref, decay_v),
                (direct_ref, direct_v),
                (bout_ref, bout_v),
                (pos_ref, pos_v),
                (fin_ref, fin_v),
                (fbias_ref, fbias_v),
                (ffreq_ref, ffreq_v),
                (fhid_ref, fhid_v),
                (wout_ref, wout_v),
            ]
        )
    ]
    consts = [
        pltpu.make_async_copy(src, dst, const_sem.at[i])
        for i, (src, dst) in enumerate(
            [
                (first_ref, first_v),
                (spin_ref, spin_v),
                (twid_ref, twid_v),
                (fwd_ref, fwd_v),
                (inv_ref, inv_v),
                (last_ref, last_v),
            ]
        )
    ]
    for copy in smalls:
        copy.start()

    bar = pltpu.get_barrier_semaphore()

    def greet(sem, to):
        pl.semaphore_signal(sem, inc=1, device_id=to, device_id_type=MESH)

    for i in range(1, CH):
        greet(bar, (s, lax.rem(c + i, CH)))
    for i in range(1, SEQ):
        greet(bar, (lax.rem(s + i, SEQ), c))

    @pl.when(jnp.logical_and(c == 0, s > 0))
    def _():
        for j in range(CH):
            greet(bar, (s - 1, j))

    for copy in smalls[:6]:
        copy.wait()
    raw[...] = jnp.zeros_like(raw)
    raw[0:3, :] = bin_v[...]
    for j in range(3):
        raw[3 + 3 * j : 6 + 3 * j, :] = taps_v[j]
    raw[12:13, :] = decay_v[...]
    raw[13:14, :] = direct_v[...]
    raw[14:15, :] = bout_v[...]

    def columns(rows, n):
        eye = (
            lax.broadcasted_iota(jnp.int32, (n, n), 0) == lax.broadcasted_iota(jnp.int32, (n, n), 1)
        ).astype(F32)
        return lax.dot_general(
            eye, rows, (((1,), (1,)), ((), ())), precision=HIGHEST, preferred_element_type=F32
        )

    prm[...] = jnp.zeros_like(prm)
    prm[:, 0:ORDER] = fout_v[...]
    prm[:, ORDER : ORDER + 16] = columns(raw[...], OWN)
    pl.semaphore_wait(bar, jnp.where(s < SEQ - 1, SEQ + CH - 1, SEQ + CH - 2))

    def put(src, dst, send, recv, to):
        pltpu.make_async_remote_copy(
            src_ref=src, dst_ref=dst, send_sem=send, recv_sem=recv, device_id=to, device_id_type=MESH
        ).start()

    def wait(ref, sem):
        pltpu.make_async_copy(ref, ref, sem).wait()

    half = pl.ds(pl.multiple_of(lax.rem(y, 2) * LANES, LANES), LANES)
    quarter = pl.ds(pl.multiple_of(y * 8, 8), 8)
    w_src = w_ref.at[:, pl.ds(pl.multiple_of((y // 2) * 16, 16), 16), half]
    w_dst = wbuf.at[:, c, y // 2, :, half]
    p_src = prm.at[quarter, :]
    p_dst = pbuf.at[c, y]
    x_dst = xc.at[rows_own, pl.ds(HALO, CHUNK)]
    h_dst = xc.at[rows_own, pl.ds(0, HALO)]

    def chunk(j):
        return x_ref.at[:, pl.ds(pl.multiple_of(j * CHUNK, CHUNK), CHUNK)]

    def tail(j):
        return x_ref.at[:, pl.ds(pl.multiple_of(j * CHUNK + CHUNK - HALO, HALO), HALO)]

    for i in range(1, CH):
        to = (s, lax.rem(c + i, CH))
        put(p_src, p_dst, s1.at[0], r1.at[0], to)
        put(w_src, w_dst, s1.at[1], r1.at[1], to)
    for i in range(1, CH):
        j = lax.rem(c + i, CH)
        put(chunk(j), x_dst, s1.at[2], r1.at[2], (s, j))
    for i in range(1, CH):
        j = lax.rem(c + i, CH)

        @pl.when(j > 0)
        def _():
            put(tail(j - 1), h_dst, s1.at[3], r1.at[3], (s, j))

    @pl.when(s < SEQ - 1)
    def _():
        put(tail(CH - 1), h_dst, s1.at[3], r1.at[3], (s + 1, 0))

    pltpu.make_async_copy(p_src, p_dst, r1.at[0]).start()
    pltpu.make_async_copy(w_src, w_dst, r1.at[1]).start()
    pltpu.make_async_copy(chunk(c), x_dst, r1.at[2]).start()

    @pl.when(c > 0)
    def _():
        pltpu.make_async_copy(tail(c - 1), h_dst, r1.at[3]).start()

    @pl.when(me == 0)
    def _():
        xc[:, 0:HALO] = jnp.zeros((D, HALO), BF16)

    for i in range(1, SEQ):
        greet(gate, (lax.rem(s + i, SEQ), c))
    for copy in consts:
        copy.start()
    for copy in smalls[6:]:
        copy.wait()

    rawnet[...] = jnp.zeros_like(rawnet)
    rawnet[0:5, :] = fin_v[...]
    rawnet[5:8, :] = fbias_v[...]
    rawnet[8:11, :] = ffreq_v[...]
    net = columns(rawnet[...], ORDER)
    here = pl.ds(pl.multiple_of(c * CHUNK, CHUNK), CHUNK)
    inner = net[:, 0:1] * pos_v[0:1, here]
    for i in range(1, 5):
        inner = inner + net[:, i : i + 1] * pos_v[i : i + 1, here]
    activity = jnp.sin(net[:, 8:9] * (inner + net[:, 5:6]))
    for layer in range(2):
        inner = (
            jnp.dot(fhid_v[layer], activity, precision=HIGHEST, preferred_element_type=F32)
            + net[:, 6 + layer : 7 + layer]
        )
        activity = jnp.sin(net[:, 9 + layer : 10 + layer] * inner)
    places = me * CHUNK + lax.broadcasted_iota(jnp.int32, (1, CHUNK), 1)
    scaled = places.astype(F32) / (LENGTH - 1)

    p_mine = pbuf.at[:, y]
    w_mine = wbuf.at[:, :, y // 2, :, half]
    wait(p_mine, r1.at[0])
    around = [(s - 2 * y + 2 * lax.rem(y + i, 4), c) for i in (1, 3, 2)]
    for to in around:
        put(p_mine, p_mine, s1.at[4], r1.at[4], to)
    wait(w_mine, r1.at[1])
    for to in around:
        put(w_mine, w_mine, s1.at[5], r1.at[5], to)

    wait(pbuf.at[pl.ds(0, 6)], r1.at[4])
    pflat[...] = pbuf[...].reshape(D, LANES)

    for lo in range(0, D, 64):
        pm = pflat[lo : lo + 64, :]
        values = jnp.dot(pm[:, 0:ORDER], activity, precision=HIGHEST, preferred_element_type=F32)
        values = values * jnp.exp(-(scaled * pm[:, DECAY : DECAY + 1]))
        for r in range(RADIX):
            stage[lo : lo + 64, r, :] = values[:, r * LANES : (r + 1) * LANES]
    ksnd[...] = stage[...].astype(BF16)

    def scatter(src, dst, at):
        send, recv = s3.at[at], r3.at[at]

        def one(si, cj):
            to = si * CH + cj
            put(src.at[to], dst.at[me], send, recv, (si, cj))

        for i in range(1, CH):
            one(s, lax.rem(c + i, CH))

        def column(i, carry):
            si = lax.rem(s + i, SEQ)
            for j in range(CH):
                one(si, lax.rem(c + j, CH))
            return carry

        lax.fori_loop(1, SEQ, column, 0)
        pltpu.make_async_copy(src.at[me], dst.at[me], recv).start()

    pl.semaphore_wait(gate, SEQ - 1)
    scatter(ksnd, krcv, 0)

    wait(xc.at[:, pl.ds(HALO, CHUNK)], r1.at[2])

    @pl.when(me > 0)
    def _():
        wait(xc.at[:, pl.ds(0, HALO)], r1.at[3])

    wait(wbuf.at[:, pl.ds(0, 6)], r1.at[5])

    for j in range(3):
        proj[j] = mm(wbuf[j].reshape(D, D), xc[...])
    column = lax.broadcasted_iota(jnp.int32, (1, HALO + CHUNK), 1)
    inside = jnp.logical_or(column >= HALO, me > 0)

    def shorts(step, carry):
        lo = pl.multiple_of(step * BLOCK, BLOCK)
        pm = pflat[pl.ds(lo, BLOCK), :]
        streams = []
        for j in range(3):
            p = jnp.where(inside, proj[j, pl.ds(lo, BLOCK), :] + pm[:, BIAS + j : BIAS + j + 1], 0.0)
            taps = [pm[:, TAPS + 3 * j + i : TAPS + 3 * j + i + 1] for i in range(3)]
            streams.append(
                taps[0] * pltpu.roll(p, 2, 1)[:, HALO:]
                + taps[1] * pltpu.roll(p, 1, 1)[:, HALO:]
                + taps[2] * p[:, HALO:]
            )
        gated = streams[2] * streams[1]
        keep0[pl.ds(lo, BLOCK), :] = streams[0]
        keepg[pl.ds(lo, BLOCK), :] = gated
        for r in range(RADIX):
            stage[pl.ds(lo, BLOCK), r, :] = gated[:, r * LANES : (r + 1) * LANES]
        return carry

    lax.fori_loop(0, D // BLOCK, shorts, 0)
    gsnd[...] = stage[...].astype(BF16)

    scatter(gsnd, grcv, 1)

    def sections(rcv):
        stage[...] = rcv[...].astype(F32)
        x = jnp.concatenate([stage[:, r, :] for r in range(RADIX)], axis=1).astype(BF16)
        for part in range(2):
            sect[part] = mm(first_v[part * D : (part + 1) * D, :], x) + mm(
                first_v[(2 + part) * D : (3 + part) * D, :], x
            )

        def ahead(step, carry):
            rows = pl.ds(pl.multiple_of(step * 32, 32), 32)
            spins = spin_v[rows, :]
            re, im = [], []
            for r in range(RADIX):
                lanes = slice(r * LANES, (r + 1) * LANES)
                a, b = sect[0, rows, lanes], sect[1, rows, lanes]
                if r:
                    cs, sn = spins[:, r : r + 1], spins[:, RADIX + r : RADIX + r + 1]
                    a, b = a * cs + b * sn, b * cs - a * sn
                re.append(a)
                im.append(b)
            e0r, e0i, e1r, e1i = re[0] + re[2], im[0] + im[2], re[0] - re[2], im[0] - im[2]
            o0r, o0i, o1r, o1i = re[1] + re[3], im[1] + im[3], re[1] - re[3], im[1] - im[3]
            outs = [
                (e0r + o0r, e0i + o0i),
                (e1r + o1i, e1i - o1r),
                (e0r - o0r, e0i - o0i),
                (e1r - o1i, e1i + o1r),
            ]
            for h, (a, b) in enumerate(outs):
                cs = twid_v[0, rows, h * LANES : (h + 1) * LANES]
                sn = twid_v[1, rows, h * LANES : (h + 1) * LANES]
                high, low = split(jnp.concatenate([a * cs + b * sn, b * cs - a * sn], axis=1))
                chi[h, rows, :] = high
                clo[h, rows, :] = low
            return carry

        lax.fori_loop(0, D // 32, ahead, 0)

    def spectrum(h):
        high, low = chi[h], clo[h]
        return mm(high, fwd_v[0]) + mm(low, fwd_v[0]) + mm(high, fwd_v[1])

    for copy in consts:
        copy.wait()
    wait(krcv, r3.at[0])
    sections(krcv)
    for h in range(RADIX):
        spec[h] = spectrum(h)
    wait(grcv, r3.at[1])
    sections(grcv)
    for h in range(RADIX):
        g, k = spectrum(h), spec[h]
        gr, gi, kr, ki = g[:, :LANES], g[:, LANES:], k[:, :LANES], k[:, LANES:]
        high, low = split(jnp.concatenate([gr * kr - gi * ki, gr * ki + gi * kr], axis=1))
        z = mm(high, inv_v[0]) + mm(low, inv_v[0]) + mm(high, inv_v[1])
        zr, zi = z[:, :LANES], z[:, LANES:]
        cs = twid_v[0, :, h * LANES : (h + 1) * LANES]
        sn = twid_v[1, :, h * LANES : (h + 1) * LANES]
        back[h, 0] = zr * cs - zi * sn
        back[h, 1] = zi * cs + zr * sn

    def behind(step, carry):
        lo = pl.multiple_of(step * 32, 32)
        rows = pl.ds(lo, 32)
        rows_im = pl.ds(pl.multiple_of(D + lo, 32), 32)
        spins = spin_v[rows, :]
        re = [back[h, 0, rows, :] for h in range(RADIX)]
        im = [back[h, 1, rows, :] for h in range(RADIX)]
        e0r, e0i, e1r, e1i = re[0] + re[2], im[0] + im[2], re[0] - re[2], im[0] - im[2]
        o0r, o0i, o1r, o1i = re[1] + re[3], im[1] + im[3], re[1] - re[3], im[1] - im[3]
        outs = [
            (e0r + o0r, e0i + o0i),
            (e1r - o1i, e1i + o1r),
            (e0r - o0r, e0i - o0i),
            (e1r + o1i, e1i - o1r),
        ]
        for r, (a, b) in enumerate(outs):
            if r:
                cs, sn = spins[:, r : r + 1], spins[:, RADIX + r : RADIX + r + 1]
                a, b = a * cs - b * sn, b * cs + a * sn
            lanes = slice(r * LANES, (r + 1) * LANES)
            high, low = split(a)
            dhi[rows, lanes] = high
            dlo[rows, lanes] = low
            high, low = split(b)
            dhi[rows_im, lanes] = high
            dlo[rows_im, lanes] = low
        return carry

    lax.fori_loop(0, D // 32, behind, 0)
    last_hi, last_lo = last_v[0:D, :], last_v[D : 2 * D, :]
    settled = mm(last_hi, dhi[...]) + mm(last_lo, dhi[...]) + mm(last_hi, dlo[...])
    for r in range(RADIX):
        stage[:, r, :] = settled[:, r * LANES : (r + 1) * LANES]
    ysnd[...] = stage[...].astype(BF16)

    scatter(ysnd, yrcv, 2)
    wait(yrcv, r3.at[2])

    stage[...] = yrcv[...].astype(F32)
    convolved = jnp.concatenate([stage[:, r, :] for r in range(RADIX)], axis=1)
    convolved = convolved + pflat[:, DIRECT : DIRECT + 1] * keepg[...]
    mixed = (keep0[...] * convolved).astype(BF16)
    osnd[...] = (mm(wout_v[...], mixed) + pflat[:, OUTB : OUTB + 1]).astype(BF16)
    o_dst = out_ref.at[:, pl.ds(pl.multiple_of(c * CHUNK, CHUNK), CHUNK)]
    for i in range(1, CH):
        j = lax.rem(c + i, CH)
        put(osnd.at[pl.ds(pl.multiple_of(j * OWN, OWN), OWN), :], o_dst, s6, r6, (s, j))
    pltpu.make_async_copy(osnd.at[rows_own, :], o_dst, r6).start()

    wait(out_ref, r6)
    most = pl.ds(0, CH - 1)
    wait(pbuf.at[most, 0], s1.at[0])
    wait(wbuf.at[:, most, 0, :, pl.ds(0, LANES)], s1.at[1])
    wait(xc.at[pl.ds(0, D - OWN), pl.ds(HALO, CHUNK)], s1.at[2])
    tails = pl.ds(0, OWN)
    wait(xc.at[pl.ds(0, 6 * OWN), pl.ds(0, HALO)], s1.at[3])

    @pl.when(c == 0)
    def _():
        wait(xc.at[tails, pl.ds(0, HALO)], s1.at[3])

    @pl.when(s < SEQ - 1)
    def _():
        wait(xc.at[tails, pl.ds(0, HALO)], s1.at[3])

    wait(pbuf.at[pl.ds(0, 6)], s1.at[4])
    wait(wbuf.at[:, pl.ds(0, 6)], s1.at[5])
    for i, buf in enumerate((ksnd, gsnd, ysnd)):
        wait(buf.at[pl.ds(0, DEV - 1)], s3.at[i])
    wait(osnd.at[pl.ds(0, D - OWN), :], s6)


def body(
    inputs,
    w_in,
    b_in,
    short_kernel,
    positional,
    filter_in,
    filter_bias,
    filter_freq,
    filter_hidden,
    filter_out,
    decay,
    conv_bias,
    w_out,
    b_out,
):
    dma = pltpu.SemaphoreType.DMA
    hbm = pl.BlockSpec(memory_space=pl.ANY)
    vmem = pltpu.VMEM
    return pl.pallas_call(
        kernel,
        out_shape=pltpu.VMEM((OWN, SPAN), BF16),
        in_specs=[hbm] * 20,
        out_specs=pl.BlockSpec(memory_space=pltpu.VMEM),
        scratch_shapes=[
            vmem((3, OWN), F32),
            vmem((3, 3, OWN), F32),
            vmem((OWN, ORDER), F32),
            vmem((1, OWN), F32),
            vmem((1, OWN), F32),
            vmem((1, OWN), F32),
            vmem((5, SPAN), F32),
            vmem((5, ORDER), F32),
            vmem((3, ORDER), F32),
            vmem((3, ORDER), F32),
            vmem((2, ORDER, ORDER), F32),
            vmem((D, D), BF16),
            vmem((16, OWN), F32),
            vmem((16, ORDER), F32),
            vmem((OWN, LANES), F32),
            vmem((D, HALO + CHUNK), BF16),
            vmem((3, CH, 2, 16, D), BF16),
            vmem((CH, 4, 8, LANES), F32),
            vmem((D, LANES), F32),
            vmem((3, D, HALO + CHUNK), F32),
            vmem((DEV, RADIX, LANES), F32),
            vmem((D, CHUNK), F32),
            vmem((D, CHUNK), F32),
            vmem((DEV, RADIX, LANES), BF16),
            vmem((DEV, RADIX, LANES), BF16),
            vmem((DEV, RADIX, LANES), BF16),
            vmem((DEV, RADIX, LANES), BF16),
            vmem((4 * D, D), BF16),
            vmem((2 * D, 2 * D), BF16),
            vmem((2, D, D), BF16),
            vmem((2, D, D), BF16),
            vmem((2, D, CHUNK), F32),
            vmem((D, LANES), F32),
            vmem((2, D, CHUNK), F32),
            vmem((RADIX, D, 2 * LANES), BF16),
            vmem((RADIX, D, 2 * LANES), BF16),
            vmem((RADIX, D, 2 * LANES), F32),
            vmem((RADIX, 2, D, LANES), F32),
            vmem((2 * D, CHUNK), BF16),
            vmem((2 * D, CHUNK), BF16),
            vmem((DEV, RADIX, LANES), BF16),
            vmem((DEV, RADIX, LANES), BF16),
            vmem((D, CHUNK), BF16),
            dma((12,)),
            dma((6,)),
            pltpu.SemaphoreType.REGULAR,
            dma((6,)),
            dma((6,)),
            dma((3,)),
            dma((3,)),
            dma,
            dma,
        ],
        compiler_params=pltpu.CompilerParams(collective_id=0, has_side_effects=True),
    )(
        inputs,
        w_in,
        b_in,
        short_kernel.transpose(0, 2, 1),
        filter_out,
        decay.reshape(1, OWN),
        conv_bias.reshape(1, OWN),
        b_out.reshape(1, OWN),
        positional,
        filter_in.T,
        filter_bias,
        filter_freq,
        filter_hidden,
        w_out,
        *tables(),
    )


def solution(mesh):
    in_specs = (
        P("ch", "seq"),
        P(None, "ch", None),
        P(None, "ch"),
        P(None, "ch", None),
        P(None, "seq"),
        P(),
        P(),
        P(),
        P(),
        P("ch", None),
        P("ch"),
        P("ch"),
        P(),
        P("ch"),
    )
    return jax.shard_map(
        body, mesh=mesh, in_specs=in_specs, out_specs=P("ch", "seq"), check_vma=False
    )
```

time: 96.7 us -> 64 us (0.66)
  Pallas kernels: 87.7 us -> 63.2 us
  local copies, waits for them, and re-layouts: 7.96 us -> 0.71 us
    pallas_call x1, Pallas kernels: 87.7 us -> 63.2 us  [body(): pl.pallas_call(kernel, out_shape=pltpu.VMEM((OWN, SPAN), BF16), in_specs=...]
    unnamed x23 -> x1, local copies, waits for them, and re-layouts: 6.84 us -> 0.71 us
where the time goes in v1:
time: 64 us; the launch traced here: 63.9 us
  Pallas kernels  63.2 us (99%)
  local copies, waits for them, and re-layouts  0.71 us (1%)
    pallas_call x1, Pallas kernels, body(): pl.pallas_call(kernel, out_shape=pltpu.VMEM((OWN, SPAN), BF16), in_specs=...  63.2 us

profile of v1, /device:TPU:1, one launch (start us, length us, event | category | flops | bytes accessed | tf_op | source)
XLA Modules:
  0.0 63.9 jit_solution(1934213017391915736)
XLA Ops:
  0.0 63.2 %shard_map.190 = bf16[32,4096]{1,0:T(8,128)(2,1)S(1)} custom-call(bf16[32,4096]{1,0:T(8,128)(2,1)} %x_ref.1, bf16[3,32,256]{2,1,0:T(8,128)(2,1)} %w_ref.1, f32[3,32]{1,0:T(4,128)} %bin_ref.1, f32[3,3,32]{2,1,0:T(4,128)} %bitcast.5, f32[32,64]{1,0:T(8,128)} %fout_ref.1, f32[1,32]{1,0:T(1,128)} %bitcast.7, f32[1,32]{1,0:T(1,128)} %bitcast.8, f32[1,32]{1,0:T(1,128)} %bitcast.9, ...), custom_call_target="tpu_custom_call" | custom-call | tf_op jit(solution)/shard_map/pallas_call | solution.py:535
  63.2 0.7 %copy.22 = bf16[32,4096]{1,0:T(8,128)(2,1)} copy(bf16[32,4096]{1,0:T(8,128)(2,1)S(1)} %shard_map.190) | data formatting | bytes 524288

commit v2 on v1

--- a/solution.py
+++ b/solution.py
@@ -24,7 +24,8 @@
 LANES = 128
 RADIX = CHUNK // LANES
 ORDER = 64
-BLOCK = 16
+FAR = (4, 3, 5, 2, 6, 1, 7)
+FARX = (2, 1, 3, 0)
 BIAS, TAPS, DECAY, DIRECT, OUTB = 64, 67, 76, 77, 78
 
 
@@ -107,7 +108,9 @@
     wbuf,
     pbuf,
     pflat,
-    proj,
+    xs,
+    cols,
+    spins,
     stage,
     keep0,
     keepg,
@@ -144,7 +147,7 @@
     s = lax.axis_index("seq")
     c = lax.axis_index("ch")
     me = s * CH + c
-    y = lax.rem(s // 2, 4)
+    px, py, pk = s // 8, lax.rem(s // 2, 4), lax.rem(s, 2)
     own = pl.multiple_of(c * OWN, OWN)
     rows_own = pl.ds(own, OWN)
 
@@ -171,8 +174,8 @@
         pltpu.make_async_copy(src, dst, const_sem.at[i])
         for i, (src, dst) in enumerate(
             [
+                (spin_ref, spin_v),
                 (first_ref, first_v),
-                (spin_ref, spin_v),
                 (twid_ref, twid_v),
                 (fwd_ref, fwd_v),
                 (inv_ref, inv_v),
@@ -229,12 +232,12 @@
     def wait(ref, sem):
         pltpu.make_async_copy(ref, ref, sem).wait()
 
-    half = pl.ds(pl.multiple_of(lax.rem(y, 2) * LANES, LANES), LANES)
-    quarter = pl.ds(pl.multiple_of(y * 8, 8), 8)
-    w_src = w_ref.at[:, pl.ds(pl.multiple_of((y // 2) * 16, 16), 16), half]
-    w_dst = wbuf.at[:, c, y // 2, :, half]
+    half = pl.ds(pl.multiple_of(lax.rem(py, 2) * LANES, LANES), LANES)
+    quarter = pl.ds(pl.multiple_of(py * 8, 8), 8)
+    w_src = w_ref.at[:, pl.ds(pl.multiple_of((py // 2) * 16, 16), 16), half]
+    w_dst = wbuf.at[:, c, py // 2, :, half]
     p_src = prm.at[quarter, :]
-    p_dst = pbuf.at[c, y]
+    p_dst = pbuf.at[c, py]
     x_dst = xc.at[rows_own, pl.ds(HALO, CHUNK)]
     h_dst = xc.at[rows_own, pl.ds(0, HALO)]
 
@@ -244,15 +247,13 @@
     def tail(j):
         return x_ref.at[:, pl.ds(pl.multiple_of(j * CHUNK + CHUNK - HALO, HALO), HALO)]
 
-    for i in range(1, CH):
-        to = (s, lax.rem(c + i, CH))
-        put(p_src, p_dst, s1.at[0], r1.at[0], to)
-        put(w_src, w_dst, s1.at[1], r1.at[1], to)
-    for i in range(1, CH):
+    for i in FAR:
+        put(p_src, p_dst, s1.at[0], r1.at[0], (s, lax.rem(c + i, CH)))
+    for i in FAR:
+        put(w_src, w_dst, s1.at[1], r1.at[1], (s, lax.rem(c + i, CH)))
+    for i in FAR:
         j = lax.rem(c + i, CH)
         put(chunk(j), x_dst, s1.at[2], r1.at[2], (s, j))
-    for i in range(1, CH):
-        j = lax.rem(c + i, CH)
 
         @pl.when(j > 0)
         def _():
@@ -300,10 +301,14 @@
     places = me * CHUNK + lax.broadcasted_iota(jnp.int32, (1, CHUNK), 1)
     scaled = places.astype(F32) / (LENGTH - 1)
 
-    p_mine = pbuf.at[:, y]
-    w_mine = wbuf.at[:, :, y // 2, :, half]
+    p_mine = pbuf.at[:, py]
+    w_mine = wbuf.at[:, :, py // 2, :, half]
+    consts[0].wait()
+    for i in range(6):
+        at = 1 + i if i < 3 else 2 + i
+        spins[i] = jnp.broadcast_to(spin_v[:, at : at + 1], (D, LANES))
     wait(p_mine, r1.at[0])
-    around = [(s - 2 * y + 2 * lax.rem(y + i, 4), c) for i in (1, 3, 2)]
+    around = [(s - 2 * py + 2 * lax.rem(py + i, 4), c) for i in (2, 1, 3)]
     for to in around:
         put(p_mine, p_mine, s1.at[4], r1.at[4], to)
     wait(w_mine, r1.at[1])
@@ -321,27 +326,42 @@
             stage[lo : lo + 64, r, :] = values[:, r * LANES : (r + 1) * LANES]
     ksnd[...] = stage[...].astype(BF16)
 
-    def scatter(src, dst, at):
+    def scatter(src, dst, at, dx):
         send, recv = s3.at[at], r3.at[at]
-
-        def one(si, cj):
-            to = si * CH + cj
-            put(src.at[to], dst.at[me], send, recv, (si, cj))
-
-        for i in range(1, CH):
-            one(s, lax.rem(c + i, CH))
-
-        def column(i, carry):
-            si = lax.rem(s + i, SEQ)
-            for j in range(CH):
-                one(si, lax.rem(c + j, CH))
+        sx = lax.rem(px + dx, 4) * 8
+
+        def ring(cj, near):
+            for dy in (2, 1, 3, 0):
+                for dk in (1, 0):
+                    if not (near and dy == 0 and dk == 0):
+                        si = sx + lax.rem(py + dy, 4) * 2 + lax.rem(pk + dk, 2)
+                        put(src.at[si * CH + cj], dst.at[me], send, recv, (si, cj))
+
+        def layer(t, carry):
+            ring(lax.rem(c + 4 + (t + 1) // 2 * (1 - 2 * lax.rem(t, 2)), CH), False)
             return carry
 
-        lax.fori_loop(1, SEQ, column, 0)
-        pltpu.make_async_copy(src.at[me], dst.at[me], recv).start()
+        if dx:
+            lax.fori_loop(0, CH, layer, 0)
+        else:
+            lax.fori_loop(0, CH - 1, layer, 0)
+            ring(c, True)
+            pltpu.make_async_copy(src.at[me], dst.at[me], recv).start()
+
+    def scatter_all(src, dst, at):
+        for dx in FARX:
+            scatter(src, dst, at, dx)
 
     pl.semaphore_wait(gate, SEQ - 1)
-    scatter(ksnd, krcv, 0)
+    scatter_all(ksnd, krcv, 0)
+
+    for j in range(3):
+        bias = jnp.broadcast_to(pflat[:, BIAS + j : BIAS + j + 1], (D, LANES))
+        for i in range(3):
+            at = TAPS + 3 * j + i
+            tap = jnp.broadcast_to(pflat[:, at : at + 1], (D, LANES))
+            cols[3 * j + i, 0] = tap
+            cols[3 * j + i, 1] = tap * bias
 
     wait(xc.at[:, pl.ds(HALO, CHUNK)], r1.at[2])
 
@@ -351,34 +371,37 @@
 
     wait(wbuf.at[:, pl.ds(0, 6)], r1.at[5])
 
-    for j in range(3):
-        proj[j] = mm(wbuf[j].reshape(D, D), xc[...])
-    column = lax.broadcasted_iota(jnp.int32, (1, HALO + CHUNK), 1)
-    inside = jnp.logical_or(column >= HALO, me > 0)
-
-    def shorts(step, carry):
-        lo = pl.multiple_of(step * BLOCK, BLOCK)
-        pm = pflat[pl.ds(lo, BLOCK), :]
-        streams = []
-        for j in range(3):
-            p = jnp.where(inside, proj[j, pl.ds(lo, BLOCK), :] + pm[:, BIAS + j : BIAS + j + 1], 0.0)
-            taps = [pm[:, TAPS + 3 * j + i : TAPS + 3 * j + i + 1] for i in range(3)]
-            streams.append(
-                taps[0] * pltpu.roll(p, 2, 1)[:, HALO:]
-                + taps[1] * pltpu.roll(p, 1, 1)[:, HALO:]
-                + taps[2] * p[:, HALO:]
-            )
-        gated = streams[2] * streams[1]
-        keep0[pl.ds(lo, BLOCK), :] = streams[0]
-        keepg[pl.ds(lo, BLOCK), :] = gated
+    wide = xc[...].astype(F32)
+    for i in (0, 1):
+        xs[i] = pltpu.roll(wide, 2 - i, 1)[:, HALO:].astype(BF16)
+    place = lax.broadcasted_iota(jnp.int32, (1, LANES), 1)
+    started = [jnp.logical_or(place >= 2 - i, me > 0).astype(F32) for i in (0, 1)]
+
+    for dx in FARX:
+        block = lax.rem(px + dx, 4)
+        lo = pl.multiple_of(block * 64, 64)
+        rows = pl.ds(lo, 64)
+        w = wbuf[:, pl.ds(block * 2, 2)].reshape(3 * 64, D)
+        taken = [mm(w, xs[0]), mm(w, xs[1]), mm(w, xc[:, HALO:])]
         for r in range(RADIX):
-            stage[pl.ds(lo, BLOCK), r, :] = gated[:, r * LANES : (r + 1) * LANES]
-        return carry
-
-    lax.fori_loop(0, D // BLOCK, shorts, 0)
-    gsnd[...] = stage[...].astype(BF16)
-
-    scatter(gsnd, grcv, 1)
+            lanes = slice(r * LANES, (r + 1) * LANES)
+            streams = []
+            for j in range(3):
+                total = None
+                for i in range(3):
+                    shifted_bias = cols[3 * j + i, 1, rows, :]
+                    if r == 0 and i < 2:
+                        shifted_bias = shifted_bias * started[i]
+                    term = cols[3 * j + i, 0, rows, :] * taken[i][64 * j : 64 * j + 64, lanes]
+                    term = term + shifted_bias
+                    total = term if total is None else total + term
+                streams.append(total)
+            gated = streams[2] * streams[1]
+            keep0[rows, lanes] = streams[0]
+            keepg[rows, lanes] = gated
+            stage[rows, r, :] = gated
+        gsnd[rows] = stage[rows].astype(BF16)
+        scatter(gsnd, grcv, 1, dx)
 
     def sections(rcv):
         stage[...] = rcv[...].astype(F32)
@@ -390,13 +413,12 @@
 
         def ahead(step, carry):
             rows = pl.ds(pl.multiple_of(step * 32, 32), 32)
-            spins = spin_v[rows, :]
             re, im = [], []
             for r in range(RADIX):
                 lanes = slice(r * LANES, (r + 1) * LANES)
                 a, b = sect[0, rows, lanes], sect[1, rows, lanes]
                 if r:
-                    cs, sn = spins[:, r : r + 1], spins[:, RADIX + r : RADIX + r + 1]
+                    cs, sn = spins[r - 1, rows, :], spins[r + 2, rows, :]
                     a, b = a * cs + b * sn, b * cs - a * sn
                 re.append(a)
                 im.append(b)
@@ -422,7 +444,7 @@
         high, low = chi[h], clo[h]
         return mm(high, fwd_v[0]) + mm(low, fwd_v[0]) + mm(high, fwd_v[1])
 
-    for copy in consts:
+    for copy in consts[1:]:
         copy.wait()
     wait(krcv, r3.at[0])
     sections(krcv)
@@ -445,7 +467,6 @@
         lo = pl.multiple_of(step * 32, 32)
         rows = pl.ds(lo, 32)
         rows_im = pl.ds(pl.multiple_of(D + lo, 32), 32)
-        spins = spin_v[rows, :]
         re = [back[h, 0, rows, :] for h in range(RADIX)]
         im = [back[h, 1, rows, :] for h in range(RADIX)]
         e0r, e0i, e1r, e1i = re[0] + re[2], im[0] + im[2], re[0] - re[2], im[0] - im[2]
@@ -458,7 +479,7 @@
         ]
         for r, (a, b) in enumerate(outs):
             if r:
-                cs, sn = spins[:, r : r + 1], spins[:, RADIX + r : RADIX + r + 1]
+                cs, sn = spins[r - 1, rows, :], spins[r + 2, rows, :]
                 a, b = a * cs - b * sn, b * cs + a * sn
             lanes = slice(r * LANES, (r + 1) * LANES)
             high, low = split(a)
@@ -476,7 +497,7 @@
         stage[:, r, :] = settled[:, r * LANES : (r + 1) * LANES]
     ysnd[...] = stage[...].astype(BF16)
 
-    scatter(ysnd, yrcv, 2)
+    scatter_all(ysnd, yrcv, 2)
     wait(yrcv, r3.at[2])
 
     stage[...] = yrcv[...].astype(F32)
@@ -485,7 +506,7 @@
     mixed = (keep0[...] * convolved).astype(BF16)
     osnd[...] = (mm(wout_v[...], mixed) + pflat[:, OUTB : OUTB + 1]).astype(BF16)
     o_dst = out_ref.at[:, pl.ds(pl.multiple_of(c * CHUNK, CHUNK), CHUNK)]
-    for i in range(1, CH):
+    for i in FAR:
         j = lax.rem(c + i, CH)
         put(osnd.at[pl.ds(pl.multiple_of(j * OWN, OWN), OWN), :], o_dst, s6, r6, (s, j))
     pltpu.make_async_copy(osnd.at[rows_own, :], o_dst, r6).start()
@@ -557,7 +578,9 @@
             vmem((3, CH, 2, 16, D), BF16),
             vmem((CH, 4, 8, LANES), F32),
             vmem((D, LANES), F32),
-            vmem((3, D, HALO + CHUNK), F32),
+            vmem((2, D, CHUNK), BF16),
+            vmem((9, 2, D, LANES), F32),
+            vmem((6, D, LANES), F32),
             vmem((DEV, RADIX, LANES), F32),
             vmem((D, CHUNK), F32),
             vmem((D, CHUNK), F32),

time: 64 us -> 59.3 us (0.927)
  Pallas kernels: 63.2 us -> 58.5 us
    pallas_call x1, Pallas kernels: 63.2 us -> 58.5 us  [body(): pl.pallas_call(kernel, out_shape=pltpu.VMEM((OWN, SPAN), BF16), in_specs=...]
where the time goes in v2:
time: 59.3 us; the launch traced here: 59.2 us
  Pallas kernels  58.5 us (99%)
  local copies, waits for them, and re-layouts  0.71 us (1%)
    pallas_call x1, Pallas kernels, body(): pl.pallas_call(kernel, out_shape=pltpu.VMEM((OWN, SPAN), BF16), in_specs=...  58.5 us

profile of v2, /device:TPU:1, one launch (start us, length us, event | category | flops | bytes accessed | tf_op | source)
XLA Modules:
  0.0 59.2 jit_solution(4465617471464962182)
XLA Ops:
  0.0 58.5 %shard_map.190 = bf16[32,4096]{1,0:T(8,128)(2,1)S(1)} custom-call(bf16[32,4096]{1,0:T(8,128)(2,1)} %x_ref.1, bf16[3,32,256]{2,1,0:T(8,128)(2,1)} %w_ref.1, f32[3,32]{1,0:T(4,128)} %bin_ref.1, f32[3,3,32]{2,1,0:T(4,128)} %bitcast.5, f32[32,64]{1,0:T(8,128)} %fout_ref.1, f32[1,32]{1,0:T(1,128)} %bitcast.7, f32[1,32]{1,0:T(1,128)} %bitcast.8, f32[1,32]{1,0:T(1,128)} %bitcast.9, ...), custom_call_target="tpu_custom_call" | custom-call | tf_op jit(solution)/shard_map/pallas_call | solution.py:556
  58.5 0.7 %copy.22 = bf16[32,4096]{1,0:T(8,128)(2,1)} copy(bf16[32,4096]{1,0:T(8,128)(2,1)S(1)} %shard_map.190) | data formatting | bytes 524288

commit v3 on v2

--- a/solution.py
+++ b/solution.py
@@ -26,7 +26,9 @@
 ORDER = 64
 FAR = (4, 3, 5, 2, 6, 1, 7)
 FARX = (2, 1, 3, 0)
-BIAS, TAPS, DECAY, DIRECT, OUTB = 64, 67, 76, 77, 78
+BIAS, TAPS, DECAY, DIRECT, OUTB = 0, 3, 12, 13, 14
+BLOCKS, WIDE = 4, 1024
+PI_HIGH, PI_LOW = 3.1414794921875, 0.00011315941810607910156
 
 
 def halves(table):
@@ -47,20 +49,32 @@
     c, s = np.cos(inner), np.sin(inner)
     forward = np.stack(halves(np.block([[c, -s], [s, c]])))
     inverse = np.stack(halves(np.block([[c, s], [-s, c]])))
-    shift = f1[:, None] + D * np.arange(RADIX)[None, :]
-    turn = 2.0 * np.pi / LENGTH * shift[:, :, None] * lanes[None, None, :]
-    turn = turn.reshape(D, CHUNK)
+    turn = 2.0 * np.pi / LENGTH * f1[:, None] * lanes[None, :]
+    step = 2.0 * np.pi / CHUNK * np.arange(RADIX)[:, None] * lanes[None, :]
     twiddle = np.stack([np.cos(turn), np.sin(turn)]).astype(np.float32)
+    steps = np.concatenate([np.cos(step), np.sin(step)]).astype(np.float32)
     spin = 2.0 * np.pi / (RADIX * D) * f1[:, None] * np.arange(RADIX)[None, :]
     spins = np.zeros((D, LANES), np.float32)
     spins[:, 0:RADIX] = np.cos(spin)
     spins[:, RADIX : 2 * RADIX] = np.sin(spin)
-    return first_stack, last_stack, forward, inverse, twiddle, spins
+    return first_stack, last_stack, forward, inverse, twiddle, steps, spins
 
 
 def split(x):
     high = x.astype(BF16)
     return high, (x - high.astype(F32)).astype(BF16)
+
+
+def sine(v):
+    turns = jnp.floor(v * (1.0 / math.pi) + 0.5)
+    rest = (v - turns * PI_HIGH) - turns * PI_LOW
+    half = turns * 0.5
+    rest = rest * (1.0 - 4.0 * (half - jnp.floor(half)))
+    square = rest * rest
+    poly = 2.6083159809786593541503e-06 * square - 0.0001981069071916863322258
+    poly = poly * square + 0.00833307858556509017944336
+    poly = poly * square - 0.166666597127914428710938
+    return rest + rest * (square * poly)
 
 
 def mm(a, b):
@@ -87,6 +101,7 @@
     fwd_ref,
     inv_ref,
     twid_ref,
+    step_ref,
     spin_ref,
     out_ref,
     bin_v,
@@ -114,6 +129,11 @@
     stage,
     keep0,
     keepg,
+    diag,
+    weight,
+    act,
+    value_v,
+    kstage,
     ksnd,
     krcv,
     gsnd,
@@ -122,8 +142,10 @@
     last_v,
     fwd_v,
     inv_v,
+    base_v,
+    step_v,
+    spin_v,
     twid_v,
-    spin_v,
     sect,
     chi,
     clo,
@@ -176,7 +198,8 @@
             [
                 (spin_ref, spin_v),
                 (first_ref, first_v),
-                (twid_ref, twid_v),
+                (twid_ref, base_v),
+                (step_ref, step_v),
                 (fwd_ref, fwd_v),
                 (inv_ref, inv_v),
                 (last_ref, last_v),
@@ -201,8 +224,8 @@
         for j in range(CH):
             greet(bar, (s - 1, j))
 
-    for copy in smalls[:6]:
-        copy.wait()
+    for i in (0, 1, 3, 4, 5):
+        smalls[i].wait()
     raw[...] = jnp.zeros_like(raw)
     raw[0:3, :] = bin_v[...]
     for j in range(3):
@@ -220,8 +243,8 @@
         )
 
     prm[...] = jnp.zeros_like(prm)
-    prm[:, 0:ORDER] = fout_v[...]
-    prm[:, ORDER : ORDER + 16] = columns(raw[...], OWN)
+    mine = columns(raw[...], OWN)
+    prm[:, 0:16] = mine
     pl.semaphore_wait(bar, jnp.where(s < SEQ - 1, SEQ + CH - 1, SEQ + CH - 2))
 
     def put(src, dst, send, recv, to):
@@ -234,8 +257,8 @@
 
     half = pl.ds(pl.multiple_of(lax.rem(py, 2) * LANES, LANES), LANES)
     quarter = pl.ds(pl.multiple_of(py * 8, 8), 8)
-    w_src = w_ref.at[:, pl.ds(pl.multiple_of((py // 2) * 16, 16), 16), half]
-    w_dst = wbuf.at[:, c, py // 2, :, half]
+    parts = ((0, pl.ds(0, 2), 2), (1, pl.ds(2, 1), 1))
+    slab = pl.ds(pl.multiple_of((py // 2) * 16, 16), 16)
     p_src = prm.at[quarter, :]
     p_dst = pbuf.at[c, py]
     x_dst = xc.at[rows_own, pl.ds(HALO, CHUNK)]
@@ -250,7 +273,18 @@
     for i in FAR:
         put(p_src, p_dst, s1.at[0], r1.at[0], (s, lax.rem(c + i, CH)))
     for i in FAR:
-        put(w_src, w_dst, s1.at[1], r1.at[1], (s, lax.rem(c + i, CH)))
+        for part, js, _ in parts:
+
+            @pl.when(pk == part)
+            def _():
+                put(
+                    w_ref.at[js, slab, half],
+                    wbuf.at[js, c, py // 2, :, half],
+                    s1.at[1],
+                    r1.at[1],
+                    (s, lax.rem(c + i, CH)),
+                )
+
     for i in FAR:
         j = lax.rem(c + i, CH)
         put(chunk(j), x_dst, s1.at[2], r1.at[2], (s, j))
@@ -264,7 +298,14 @@
         put(tail(CH - 1), h_dst, s1.at[3], r1.at[3], (s + 1, 0))
 
     pltpu.make_async_copy(p_src, p_dst, r1.at[0]).start()
-    pltpu.make_async_copy(w_src, w_dst, r1.at[1]).start()
+    for part, js, _ in parts:
+
+        @pl.when(pk == part)
+        def _():
+            pltpu.make_async_copy(
+                w_ref.at[js, slab, half], wbuf.at[js, c, py // 2, :, half], r1.at[1]
+            ).start()
+
     pltpu.make_async_copy(chunk(c), x_dst, r1.at[2]).start()
 
     @pl.when(c > 0)
@@ -279,81 +320,143 @@
         greet(gate, (lax.rem(s + i, SEQ), c))
     for copy in consts:
         copy.start()
-    for copy in smalls[6:]:
-        copy.wait()
+    for i in (2, 6, 7, 8, 9, 10, 11):
+        smalls[i].wait()
 
     rawnet[...] = jnp.zeros_like(rawnet)
     rawnet[0:5, :] = fin_v[...]
     rawnet[5:8, :] = fbias_v[...]
     rawnet[8:11, :] = ffreq_v[...]
     net = columns(rawnet[...], ORDER)
-    here = pl.ds(pl.multiple_of(c * CHUNK, CHUNK), CHUNK)
-    inner = net[:, 0:1] * pos_v[0:1, here]
-    for i in range(1, 5):
-        inner = inner + net[:, i : i + 1] * pos_v[i : i + 1, here]
-    activity = jnp.sin(net[:, 8:9] * (inner + net[:, 5:6]))
-    for layer in range(2):
-        inner = (
-            jnp.dot(fhid_v[layer], activity, precision=HIGHEST, preferred_element_type=F32)
-            + net[:, 6 + layer : 7 + layer]
+    diag[...] = jnp.zeros_like(diag)
+    for b in range(BLOCKS):
+        at = slice(b * ORDER, (b + 1) * ORDER)
+        diag[0, at, at] = fhid_v[0]
+        diag[1, at, at] = fhid_v[1]
+        diag[2, b * OWN : (b + 1) * OWN, at] = fout_v[...]
+    for i in range(3):
+        high, low = split(diag[i])
+        weight[i, 0:D] = high
+        weight[i, D : 2 * D] = low
+
+    def tile(step):
+        b, side = step // 2, lax.rem(step, 2)
+        rows = pl.ds(pl.multiple_of(b * ORDER, ORDER), ORDER)
+        return b, side, rows, pl.ds(pl.multiple_of(side * CHUNK, CHUNK), CHUNK)
+
+    def keep(layer, value, rows, lanes):
+        high, low = split(
+            sine(net[:, 8 + layer : 9 + layer] * (value + net[:, 5 + layer : 6 + layer]))
         )
-        activity = jnp.sin(net[:, 9 + layer : 10 + layer] * inner)
-    places = me * CHUNK + lax.broadcasted_iota(jnp.int32, (1, CHUNK), 1)
-    scaled = places.astype(F32) / (LENGTH - 1)
+        act[0, rows, lanes] = high
+        act[1, rows, lanes] = low
+
+    def enter(step, carry):
+        b, side, rows, lanes = tile(step)
+        here = pl.ds(pl.multiple_of(step * CHUNK, CHUNK), CHUNK)
+        value = net[:, 0:1] * pos_v[0:1, here]
+        for i in range(1, 5):
+            value = value + net[:, i : i + 1] * pos_v[i : i + 1, here]
+        keep(0, value, rows, lanes)
+        return carry
+
+    lax.fori_loop(0, 2 * BLOCKS, enter, 0)
+
+    def product(i, n):
+        both, one = weight[i, 0 : D + n], weight[i, 0:n]
+        wide = mm(both, act[0])
+        return wide[0:n] + wide[D : D + n] + mm(one, act[1])
+
+    def hidden(layer):
+        value_v[...] = product(layer - 1, D)
+
+        def leave(step, carry):
+            b, side, rows, lanes = tile(step)
+            keep(layer, value_v[rows, lanes], rows, lanes)
+            return carry
+
+        lax.fori_loop(0, 2 * BLOCKS, leave, 0)
+
+    hidden(1)
 
     p_mine = pbuf.at[:, py]
-    w_mine = wbuf.at[:, :, py // 2, :, half]
-    consts[0].wait()
-    for i in range(6):
-        at = 1 + i if i < 3 else 2 + i
-        spins[i] = jnp.broadcast_to(spin_v[:, at : at + 1], (D, LANES))
     wait(p_mine, r1.at[0])
     around = [(s - 2 * py + 2 * lax.rem(py + i, 4), c) for i in (2, 1, 3)]
     for to in around:
         put(p_mine, p_mine, s1.at[4], r1.at[4], to)
-    wait(w_mine, r1.at[1])
-    for to in around:
-        put(w_mine, w_mine, s1.at[5], r1.at[5], to)
+    for part, js, _ in parts:
+
+        @pl.when(pk == part)
+        def _():
+            w_mine = wbuf.at[js, :, py // 2, :, half]
+            wait(w_mine, r1.at[1])
+            for to in around:
+                put(w_mine, w_mine, s1.at[5], r1.at[5], to)
+
+    hidden(2)
+    values = product(2, BLOCKS * OWN)
+    lane = lax.broadcasted_iota(jnp.int32, (1, WIDE), 1)
+    for b in range(BLOCKS):
+        places = s * SPAN + b * WIDE + lane
+        scaled = places.astype(F32) / (LENGTH - 1)
+        window = jnp.exp(-(scaled * mine[:, DECAY : DECAY + 1]))
+        block = values[b * OWN : (b + 1) * OWN] * window
+        for q in range(2 * RADIX):
+            kstage[:, 2 * b + q // RADIX, q % RADIX, :] = block[:, q * LANES : (q + 1) * LANES]
+    ksnd[...] = kstage[...].astype(BF16)
+    far = [(i, j, l) for i in (2, 1, 3, 0) for j in (2, 1, 3, 0) for l in (1, 0)]
+    theirs = pl.ds(pl.multiple_of(s * CH, CH), CH)
+    for i, j, l in far[:-1]:
+        si = lax.rem(px + i, 4) * 8 + lax.rem(py + j, 4) * 2 + lax.rem(pk + l, 2)
+        put(ksnd.at[si], krcv.at[theirs], s3.at[0], r3.at[0], (si, c))
+    pltpu.make_async_copy(ksnd.at[s], krcv.at[theirs], r3.at[0]).start()
 
     wait(pbuf.at[pl.ds(0, 6)], r1.at[4])
     pflat[...] = pbuf[...].reshape(D, LANES)
-
-    for lo in range(0, D, 64):
-        pm = pflat[lo : lo + 64, :]
-        values = jnp.dot(pm[:, 0:ORDER], activity, precision=HIGHEST, preferred_element_type=F32)
-        values = values * jnp.exp(-(scaled * pm[:, DECAY : DECAY + 1]))
-        for r in range(RADIX):
-            stage[lo : lo + 64, r, :] = values[:, r * LANES : (r + 1) * LANES]
-    ksnd[...] = stage[...].astype(BF16)
-
-    def scatter(src, dst, at, dx):
+    for part, js, n in parts:
+
+        @pl.when(pk == part)
+        def _():
+            wait(wbuf.at[js, pl.ds(0, 6)], r1.at[5])
+            put(wbuf.at[js], wbuf.at[js], s1.at[6], r1.at[6], (s + 1 - 2 * pk, c))
+
+    for copy in consts:
+        copy.wait()
+    for i in range(6):
+        at = 1 + i if i < 3 else 2 + i
+        spins[i] = jnp.broadcast_to(spin_v[:, at : at + 1], (D, LANES))
+    for h in range(RADIX):
+        lanes = slice(h * LANES, (h + 1) * LANES)
+        cs, sn = step_v[h : h + 1, :], step_v[RADIX + h : RADIX + h + 1, :]
+        twid_v[0, :, lanes] = base_v[0] * cs - base_v[1] * sn
+        twid_v[1, :, lanes] = base_v[1] * cs + base_v[0] * sn
+
+    def scatter(src, dst, row, at, dz, by_channel):
         send, recv = s3.at[at], r3.at[at]
-        sx = lax.rem(px + dx, 4) * 8
-
-        def ring(cj, near):
+        pair = 2 * lax.rem(c // 2 + dz, 4)
+        odd = lax.rem(c, 2)
+        planes = (pair + 1 - odd, pair + odd)
+
+        def ring(dx, near):
+            sx = lax.rem(px + dx, 4) * 8
             for dy in (2, 1, 3, 0):
                 for dk in (1, 0):
-                    if not (near and dy == 0 and dk == 0):
-                        si = sx + lax.rem(py + dy, 4) * 2 + lax.rem(pk + dk, 2)
-                        put(src.at[si * CH + cj], dst.at[me], send, recv, (si, cj))
+                    si = sx + lax.rem(py + dy, 4) * 2 + lax.rem(pk + dk, 2)
+                    for cj in planes[: 1 if near and dy == 0 and dk == 0 else 2]:
+                        at_src = cj * SEQ + si if by_channel else si * CH + cj
+                        put(src.at[at_src], dst.at[row], send, recv, (si, cj))
 
         def layer(t, carry):
-            ring(lax.rem(c + 4 + (t + 1) // 2 * (1 - 2 * lax.rem(t, 2)), CH), False)
+            ring(2 + (t + 1) // 2 * (1 - 2 * lax.rem(t, 2)), False)
             return carry
 
-        if dx:
-            lax.fori_loop(0, CH, layer, 0)
+        if dz:
+            lax.fori_loop(0, 4, layer, 0)
         else:
-            lax.fori_loop(0, CH - 1, layer, 0)
-            ring(c, True)
-            pltpu.make_async_copy(src.at[me], dst.at[me], recv).start()
-
-    def scatter_all(src, dst, at):
-        for dx in FARX:
-            scatter(src, dst, at, dx)
-
-    pl.semaphore_wait(gate, SEQ - 1)
-    scatter_all(ksnd, krcv, 0)
+            lax.fori_loop(0, 3, layer, 0)
+            ring(0, True)
+            at_src = c * SEQ + s if by_channel else me
+            pltpu.make_async_copy(src.at[at_src], dst.at[row], recv).start()
 
     for j in range(3):
         bias = jnp.broadcast_to(pflat[:, BIAS + j : BIAS + j + 1], (D, LANES))
@@ -363,13 +466,18 @@
             cols[3 * j + i, 0] = tap
             cols[3 * j + i, 1] = tap * bias
 
+    pl.semaphore_wait(gate, SEQ - 1)
     wait(xc.at[:, pl.ds(HALO, CHUNK)], r1.at[2])
 
     @pl.when(me > 0)
     def _():
         wait(xc.at[:, pl.ds(0, HALO)], r1.at[3])
 
-    wait(wbuf.at[:, pl.ds(0, 6)], r1.at[5])
+    for part, js, _ in parts:
+
+        @pl.when(pk != part)
+        def _():
+            wait(wbuf.at[js], r1.at[6])
 
     wide = xc[...].astype(F32)
     for i in (0, 1):
@@ -377,8 +485,8 @@
     place = lax.broadcasted_iota(jnp.int32, (1, LANES), 1)
     started = [jnp.logical_or(place >= 2 - i, me > 0).astype(F32) for i in (0, 1)]
 
-    for dx in FARX:
-        block = lax.rem(px + dx, 4)
+    for dz in FARX:
+        block = lax.rem(c // 2 + dz, 4)
         lo = pl.multiple_of(block * 64, 64)
         rows = pl.ds(lo, 64)
         w = wbuf[:, pl.ds(block * 2, 2)].reshape(3 * 64, D)
@@ -401,7 +509,7 @@
             keepg[rows, lanes] = gated
             stage[rows, r, :] = gated
         gsnd[rows] = stage[rows].astype(BF16)
-        scatter(gsnd, grcv, 1, dx)
+        scatter(gsnd, grcv, me, 1, dz, True)
 
     def sections(rcv):
         stage[...] = rcv[...].astype(F32)
@@ -444,8 +552,6 @@
         high, low = chi[h], clo[h]
         return mm(high, fwd_v[0]) + mm(low, fwd_v[0]) + mm(high, fwd_v[1])
 
-    for copy in consts[1:]:
-        copy.wait()
     wait(krcv, r3.at[0])
     sections(krcv)
     for h in range(RADIX):
@@ -497,7 +603,8 @@
         stage[:, r, :] = settled[:, r * LANES : (r + 1) * LANES]
     ysnd[...] = stage[...].astype(BF16)
 
-    scatter_all(ysnd, yrcv, 2)
+    for dz in FARX:
+        scatter(ysnd, yrcv, c * SEQ + s, 2, dz, False)
     wait(yrcv, r3.at[2])
 
     stage[...] = yrcv[...].astype(F32)
@@ -514,7 +621,14 @@
     wait(out_ref, r6)
     most = pl.ds(0, CH - 1)
     wait(pbuf.at[most, 0], s1.at[0])
-    wait(wbuf.at[:, most, 0, :, pl.ds(0, LANES)], s1.at[1])
+    for part, js, _ in parts:
+
+        @pl.when(pk == part)
+        def _():
+            wait(wbuf.at[js, most, 0, :, pl.ds(0, LANES)], s1.at[1])
+            wait(wbuf.at[js, pl.ds(0, 6)], s1.at[5])
+            wait(wbuf.at[js], s1.at[6])
+
     wait(xc.at[pl.ds(0, D - OWN), pl.ds(HALO, CHUNK)], s1.at[2])
     tails = pl.ds(0, OWN)
     wait(xc.at[pl.ds(0, 6 * OWN), pl.ds(0, HALO)], s1.at[3])
@@ -528,8 +642,8 @@
         wait(xc.at[tails, pl.ds(0, HALO)], s1.at[3])
 
     wait(pbuf.at[pl.ds(0, 6)], s1.at[4])
-    wait(wbuf.at[:, pl.ds(0, 6)], s1.at[5])
-    for i, buf in enumerate((ksnd, gsnd, ysnd)):
+    wait(ksnd.at[pl.ds(0, SEQ - 1)], s3.at[0])
+    for i, buf in ((1, gsnd), (2, ysnd)):
         wait(buf.at[pl.ds(0, DEV - 1)], s3.at[i])
     wait(osnd.at[pl.ds(0, D - OWN), :], s6)
 
@@ -556,7 +670,7 @@
     return pl.pallas_call(
         kernel,
         out_shape=pltpu.VMEM((OWN, SPAN), BF16),
-        in_specs=[hbm] * 20,
+        in_specs=[hbm] * 21,
         out_specs=pl.BlockSpec(memory_space=pltpu.VMEM),
         scratch_shapes=[
             vmem((3, OWN), F32),
@@ -584,7 +698,12 @@
             vmem((DEV, RADIX, LANES), F32),
             vmem((D, CHUNK), F32),
             vmem((D, CHUNK), F32),
-            vmem((DEV, RADIX, LANES), BF16),
+            vmem((3, D, D), F32),
+            vmem((3, 2 * D, D), BF16),
+            vmem((2, D, WIDE), BF16),
+            vmem((D, WIDE), F32),
+            vmem((OWN, CH, RADIX, LANES), F32),
+            vmem((OWN, CH, RADIX, LANES), BF16),
             vmem((DEV, RADIX, LANES), BF16),
             vmem((DEV, RADIX, LANES), BF16),
             vmem((DEV, RADIX, LANES), BF16),
@@ -592,8 +711,10 @@
             vmem((2 * D, 2 * D), BF16),
             vmem((2, D, D), BF16),
             vmem((2, D, D), BF16),
+            vmem((2, D, LANES), F32),
+            vmem((2 * RADIX, LANES), F32),
+            vmem((D, LANES), F32),
             vmem((2, D, CHUNK), F32),
-            vmem((D, LANES), F32),
             vmem((2, D, CHUNK), F32),
             vmem((RADIX, D, 2 * LANES), BF16),
             vmem((RADIX, D, 2 * LANES), BF16),
@@ -605,10 +726,10 @@
             vmem((DEV, RADIX, LANES), BF16),
             vmem((D, CHUNK), BF16),
             dma((12,)),
-            dma((6,)),
+            dma((7,)),
             pltpu.SemaphoreType.REGULAR,
-            dma((6,)),
-            dma((6,)),
+            dma((7,)),
+            dma((7,)),
             dma((3,)),
             dma((3,)),
             dma,

time: 59.3 us -> 58 us (0.978)
  Pallas kernels: 58.5 us -> 57.2 us
    pallas_call x1, Pallas kernels: 58.5 us -> 57.2 us  [body(): pl.pallas_call(kernel, out_shape=pltpu.VMEM((OWN, SPAN), BF16), in_specs=...]
where the time goes in v3:
time: 58 us; the launch traced here: 57.9 us
  Pallas kernels  57.2 us (99%)
  local copies, waits for them, and re-layouts  0.71 us (1%)
    pallas_call x1, Pallas kernels, body(): pl.pallas_call(kernel, out_shape=pltpu.VMEM((OWN, SPAN), BF16), in_specs=...  57.2 us

profile of v3, /device:TPU:1, one launch (start us, length us, event | category | flops | bytes accessed | tf_op | source)
XLA Modules:
  0.0 57.9 jit_solution(10063381934856795700)
XLA Ops:
  0.0 57.2 %shard_map.199 = bf16[32,4096]{1,0:T(8,128)(2,1)S(1)} custom-call(bf16[32,4096]{1,0:T(8,128)(2,1)} %x_ref.1, bf16[3,32,256]{2,1,0:T(8,128)(2,1)} %w_ref.1, f32[3,32]{1,0:T(4,128)} %bin_ref.1, f32[3,3,32]{2,1,0:T(4,128)} %bitcast.5, f32[32,64]{1,0:T(8,128)} %fout_ref.1, f32[1,32]{1,0:T(1,128)} %bitcast.7, f32[1,32]{1,0:T(1,128)} %bitcast.8, f32[1,32]{1,0:T(1,128)} %bitcast.9, ...), custom_call_target="tpu_custom_call" | custom-call | tf_op jit(solution)/shard_map/pallas_call | solution.py:670
  57.2 0.7 %copy.23 = bf16[32,4096]{1,0:T(8,128)(2,1)} copy(bf16[32,4096]{1,0:T(8,128)(2,1)S(1)} %shard_map.199) | data formatting | bytes 524288

commit v4 on v3

--- a/solution.py
+++ b/solution.py
@@ -24,8 +24,9 @@
 LANES = 128
 RADIX = CHUNK // LANES
 ORDER = 64
+HALF = CHUNK // 2
+PAIR = RADIX // 2
 FAR = (4, 3, 5, 2, 6, 1, 7)
-FARX = (2, 1, 3, 0)
 BIAS, TAPS, DECAY, DIRECT, OUTB = 0, 3, 12, 13, 14
 BLOCKS, WIDE = 4, 1024
 PI_HIGH, PI_LOW = 3.1414794921875, 0.00011315941810607910156
@@ -127,6 +128,7 @@
     cols,
     spins,
     stage,
+    stage2,
     keep0,
     keepg,
     diag,
@@ -158,6 +160,7 @@
     osnd,
     small_sem,
     const_sem,
+    ring_sem,
     gate,
     s1,
     r1,
@@ -170,6 +173,7 @@
     c = lax.axis_index("ch")
     me = s * CH + c
     px, py, pk = s // 8, lax.rem(s // 2, 4), lax.rem(s, 2)
+    quad = py + pk * (px - py)
     own = pl.multiple_of(c * OWN, OWN)
     rows_own = pl.ds(own, OWN)
 
@@ -255,12 +259,13 @@
     def wait(ref, sem):
         pltpu.make_async_copy(ref, ref, sem).wait()
 
-    half = pl.ds(pl.multiple_of(lax.rem(py, 2) * LANES, LANES), LANES)
-    quarter = pl.ds(pl.multiple_of(py * 8, 8), 8)
-    parts = ((0, pl.ds(0, 2), 2), (1, pl.ds(2, 1), 1))
-    slab = pl.ds(pl.multiple_of((py // 2) * 16, 16), 16)
+    half = pl.ds(pl.multiple_of(lax.rem(quad, 2) * LANES, LANES), LANES)
+    quarter = pl.ds(pl.multiple_of(quad * 8, 8), 8)
+    octet = 2 * pk + quad // 2
+    w_src = w_ref.at[:, pl.ds(pl.multiple_of(octet * 8, 8), 8), half]
+    w_dst = wbuf.at[:, c, octet, :, half]
     p_src = prm.at[quarter, :]
-    p_dst = pbuf.at[c, py]
+    p_dst = pbuf.at[c, quad]
     x_dst = xc.at[rows_own, pl.ds(HALO, CHUNK)]
     h_dst = xc.at[rows_own, pl.ds(0, HALO)]
 
@@ -273,17 +278,11 @@
     for i in FAR:
         put(p_src, p_dst, s1.at[0], r1.at[0], (s, lax.rem(c + i, CH)))
     for i in FAR:
-        for part, js, _ in parts:
-
-            @pl.when(pk == part)
-            def _():
-                put(
-                    w_ref.at[js, slab, half],
-                    wbuf.at[js, c, py // 2, :, half],
-                    s1.at[1],
-                    r1.at[1],
-                    (s, lax.rem(c + i, CH)),
-                )
+        put(w_src, w_dst, s1.at[1], r1.at[1], (s, lax.rem(c + i, CH)))
+
+    @pl.when(s < SEQ - 1)
+    def _():
+        put(tail(CH - 1), h_dst, s1.at[3], r1.at[3], (s + 1, 0))
 
     for i in FAR:
         j = lax.rem(c + i, CH)
@@ -293,19 +292,9 @@
         def _():
             put(tail(j - 1), h_dst, s1.at[3], r1.at[3], (s, j))
 
-    @pl.when(s < SEQ - 1)
-    def _():
-        put(tail(CH - 1), h_dst, s1.at[3], r1.at[3], (s + 1, 0))
 
     pltpu.make_async_copy(p_src, p_dst, r1.at[0]).start()
-    for part, js, _ in parts:
-
-        @pl.when(pk == part)
-        def _():
-            pltpu.make_async_copy(
-                w_ref.at[js, slab, half], wbuf.at[js, c, py // 2, :, half], r1.at[1]
-            ).start()
-
+    pltpu.make_async_copy(w_src, w_dst, r1.at[1]).start()
     pltpu.make_async_copy(chunk(c), x_dst, r1.at[2]).start()
 
     @pl.when(c > 0)
@@ -379,19 +368,23 @@
 
     hidden(1)
 
-    p_mine = pbuf.at[:, py]
+    ring = 2 + 6 * pk
+    around = [(i, (s + ring * (lax.rem(quad + i, 4) - quad), c)) for i in (2, 1, 3)]
+    partner = (s + 1 - 2 * pk, c)
+
+    def piece(q):
+        lanes = pl.ds(pl.multiple_of(lax.rem(q, 2) * LANES, LANES), LANES)
+        return wbuf.at[:, :, 2 * pk + q // 2, :, lanes]
+
+    p_mine = pbuf.at[:, quad]
     wait(p_mine, r1.at[0])
-    around = [(s - 2 * py + 2 * lax.rem(py + i, 4), c) for i in (2, 1, 3)]
-    for to in around:
+    for _, to in around:
         put(p_mine, p_mine, s1.at[4], r1.at[4], to)
-    for part, js, _ in parts:
-
-        @pl.when(pk == part)
-        def _():
-            w_mine = wbuf.at[js, :, py // 2, :, half]
-            wait(w_mine, r1.at[1])
-            for to in around:
-                put(w_mine, w_mine, s1.at[5], r1.at[5], to)
+    w_mine = piece(quad)
+    wait(w_mine, r1.at[1])
+    for i, to in around:
+        put(w_mine, w_mine, s1.at[5], ring_sem.at[i - 1], to)
+    put(w_mine, w_mine, s1.at[6], r1.at[6], partner)
 
     hidden(2)
     values = product(2, BLOCKS * OWN)
@@ -411,15 +404,13 @@
         put(ksnd.at[si], krcv.at[theirs], s3.at[0], r3.at[0], (si, c))
     pltpu.make_async_copy(ksnd.at[s], krcv.at[theirs], r3.at[0]).start()
 
-    wait(pbuf.at[pl.ds(0, 6)], r1.at[4])
-    pflat[...] = pbuf[...].reshape(D, LANES)
-    for part, js, n in parts:
-
-        @pl.when(pk == part)
-        def _():
-            wait(wbuf.at[js, pl.ds(0, 6)], r1.at[5])
-            put(wbuf.at[js], wbuf.at[js], s1.at[6], r1.at[6], (s + 1 - 2 * pk, c))
-
+    def hand_over(i):
+        got = piece(lax.rem(quad + 4 - i, 4))
+        wait(got, ring_sem.at[i - 1])
+        put(got, got, s1.at[6], r1.at[6], partner)
+
+    hand_over(1)
+    hand_over(3)
     for copy in consts:
         copy.wait()
     for i in range(6):
@@ -431,33 +422,16 @@
         twid_v[0, :, lanes] = base_v[0] * cs - base_v[1] * sn
         twid_v[1, :, lanes] = base_v[1] * cs + base_v[0] * sn
 
-    def scatter(src, dst, row, at, dz, by_channel):
-        send, recv = s3.at[at], r3.at[at]
-        pair = 2 * lax.rem(c // 2 + dz, 4)
-        odd = lax.rem(c, 2)
-        planes = (pair + 1 - odd, pair + odd)
-
-        def ring(dx, near):
-            sx = lax.rem(px + dx, 4) * 8
-            for dy in (2, 1, 3, 0):
-                for dk in (1, 0):
-                    si = sx + lax.rem(py + dy, 4) * 2 + lax.rem(pk + dk, 2)
-                    for cj in planes[: 1 if near and dy == 0 and dk == 0 else 2]:
-                        at_src = cj * SEQ + si if by_channel else si * CH + cj
-                        put(src.at[at_src], dst.at[row], send, recv, (si, cj))
-
-        def layer(t, carry):
-            ring(2 + (t + 1) // 2 * (1 - 2 * lax.rem(t, 2)), False)
-            return carry
-
-        if dz:
-            lax.fori_loop(0, 4, layer, 0)
-        else:
-            lax.fori_loop(0, 3, layer, 0)
-            ring(0, True)
-            at_src = c * SEQ + s if by_channel else me
-            pltpu.make_async_copy(src.at[at_src], dst.at[row], recv).start()
-
+    spots = [(i, j, l) for i in range(4) for j in range(4) for l in range(2)]
+    spots.sort(key=lambda o: -(min(o[0], 4 - o[0]) + min(o[1], 4 - o[1])))
+    spots = [o for o in spots if o != (0, 0, 0)] + [(0, 0, 0)]
+    at_x = [lax.rem(px + i, 4) * 8 for i in range(4)]
+    at_y = [lax.rem(py + i, 4) * 2 for i in range(4)]
+    at_k = [lax.rem(pk + i, 2) for i in range(2)]
+
+    hand_over(2)
+    wait(pbuf.at[pl.ds(0, 6)], r1.at[4])
+    pflat[...] = pbuf[...].reshape(D, LANES)
     for j in range(3):
         bias = jnp.broadcast_to(pflat[:, BIAS + j : BIAS + j + 1], (D, LANES))
         for i in range(3):
@@ -473,11 +447,7 @@
     def _():
         wait(xc.at[:, pl.ds(0, HALO)], r1.at[3])
 
-    for part, js, _ in parts:
-
-        @pl.when(pk != part)
-        def _():
-            wait(wbuf.at[js], r1.at[6])
+    wait(wbuf.at[:, :, pl.ds(0, 2)], r1.at[6])
 
     wide = xc[...].astype(F32)
     for i in (0, 1):
@@ -485,11 +455,10 @@
     place = lax.broadcasted_iota(jnp.int32, (1, LANES), 1)
     started = [jnp.logical_or(place >= 2 - i, me > 0).astype(F32) for i in (0, 1)]
 
-    for dz in FARX:
-        block = lax.rem(c // 2 + dz, 4)
-        lo = pl.multiple_of(block * 64, 64)
-        rows = pl.ds(lo, 64)
-        w = wbuf[:, pl.ds(block * 2, 2)].reshape(3 * 64, D)
+    def gates(t, carry):
+        pair = lax.rem(c // 2 + 2 + (t + 1) // 2 * (1 - 2 * lax.rem(t, 2)), 4)
+        rows = pl.ds(pl.multiple_of(pair * 64, 64), 64)
+        w = wbuf[:, pl.ds(pair * 2, 2)].astype(F32).reshape(3 * 64, D).astype(BF16)
         taken = [mm(w, xs[0]), mm(w, xs[1]), mm(w, xc[:, HALO:])]
         for r in range(RADIX):
             lanes = slice(r * LANES, (r + 1) * LANES)
@@ -509,9 +478,28 @@
             keepg[rows, lanes] = gated
             stage[rows, r, :] = gated
         gsnd[rows] = stage[rows].astype(BF16)
-        scatter(gsnd, grcv, me, 1, dz, True)
-
-    def sections(rcv):
+        for i, j, l in spots:
+            si = at_x[i] + at_y[j] + at_k[l]
+            for e in range(2):
+                cj = 2 * pair + e
+                src, dst = gsnd.at[cj * SEQ + si], grcv.at[me]
+                if (i, j, l) == (0, 0, 0):
+
+                    @pl.when(cj != c)
+                    def _():
+                        put(src, dst, s3.at[1], r3.at[1], (si, cj))
+
+                    @pl.when(cj == c)
+                    def _():
+                        pltpu.make_async_copy(src, dst, r3.at[1]).start()
+
+                else:
+                    put(src, dst, s3.at[1], r3.at[1], (si, cj))
+        return carry
+
+    lax.fori_loop(0, 4, gates, 0)
+
+    def whole(rcv):
         stage[...] = rcv[...].astype(F32)
         x = jnp.concatenate([stage[:, r, :] for r in range(RADIX)], axis=1).astype(BF16)
         for part in range(2):
@@ -519,6 +507,7 @@
                 first_v[(2 + part) * D : (3 + part) * D, :], x
             )
 
+    def turned():
         def ahead(step, carry):
             rows = pl.ds(pl.multiple_of(step * 32, 32), 32)
             re, im = [], []
@@ -553,11 +542,13 @@
         return mm(high, fwd_v[0]) + mm(low, fwd_v[0]) + mm(high, fwd_v[1])
 
     wait(krcv, r3.at[0])
-    sections(krcv)
+    whole(krcv)
+    turned()
     for h in range(RADIX):
         spec[h] = spectrum(h)
     wait(grcv, r3.at[1])
-    sections(grcv)
+    whole(grcv)
+    turned()
     for h in range(RADIX):
         g, k = spectrum(h), spec[h]
         gr, gi, kr, ki = g[:, :LANES], g[:, LANES:], k[:, :LANES], k[:, LANES:]
@@ -598,37 +589,61 @@
 
     lax.fori_loop(0, D // 32, behind, 0)
     last_hi, last_lo = last_v[0:D, :], last_v[D : 2 * D, :]
-    settled = mm(last_hi, dhi[...]) + mm(last_lo, dhi[...]) + mm(last_hi, dlo[...])
-    for r in range(RADIX):
-        stage[:, r, :] = settled[:, r * LANES : (r + 1) * LANES]
-    ysnd[...] = stage[...].astype(BF16)
-
-    for dz in FARX:
-        scatter(ysnd, yrcv, c * SEQ + s, 2, dz, False)
-    wait(yrcv, r3.at[2])
-
-    stage[...] = yrcv[...].astype(F32)
-    convolved = jnp.concatenate([stage[:, r, :] for r in range(RADIX)], axis=1)
-    convolved = convolved + pflat[:, DIRECT : DIRECT + 1] * keepg[...]
-    mixed = (keep0[...] * convolved).astype(BF16)
-    osnd[...] = (mm(wout_v[...], mixed) + pflat[:, OUTB : OUTB + 1]).astype(BF16)
-    o_dst = out_ref.at[:, pl.ds(pl.multiple_of(c * CHUNK, CHUNK), CHUNK)]
-    for i in FAR:
-        j = lax.rem(c + i, CH)
-        put(osnd.at[pl.ds(pl.multiple_of(j * OWN, OWN), OWN), :], o_dst, s6, r6, (s, j))
-    pltpu.make_async_copy(osnd.at[rows_own, :], o_dst, r6).start()
-
-    wait(out_ref, r6)
+    def settle(h, carry):
+        lanes_h = pl.ds(pl.multiple_of(h * HALF, HALF), HALF)
+        high, low = dhi[:, lanes_h], dlo[:, lanes_h]
+        settled = mm(last_hi, high) + mm(last_lo, high) + mm(last_hi, low)
+        for r in range(PAIR):
+            stage2[:, r, :] = settled[:, r * LANES : (r + 1) * LANES]
+        ysnd[h] = stage2[...].astype(BF16)
+        to_row = c * SEQ + s
+        for i, j, l in spots:
+            si = at_x[i] + at_y[j] + at_k[l]
+            for far in FAR + (0,):
+                if (i, j, l, far) != (0, 0, 0, 0):
+                    cj = lax.rem(c + far, CH)
+                    put(
+                        ysnd.at[h, si * CH + cj],
+                        yrcv.at[h, to_row],
+                        s3.at[3 + h],
+                        r3.at[3 + h],
+                        (si, cj),
+                    )
+        pltpu.make_async_copy(ysnd.at[h, me], yrcv.at[h, to_row], r3.at[3 + h]).start()
+        return carry
+
+    lax.fori_loop(0, 2, settle, 0)
+
+    def mix(h):
+        wait(yrcv.at[h], r3.at[3 + h])
+        cols_h = slice(h * HALF, (h + 1) * HALF)
+        stage2[...] = yrcv[h].astype(F32)
+        convolved = jnp.concatenate([stage2[:, r, :] for r in range(PAIR)], axis=1)
+        convolved = convolved + pflat[:, DIRECT : DIRECT + 1] * keepg[:, cols_h]
+        mixed = (keep0[:, cols_h] * convolved).astype(BF16)
+        osnd[h] = (mm(wout_v[...], mixed) + pflat[:, OUTB : OUTB + 1]).astype(BF16)
+        o_dst = out_ref.at[:, pl.ds(pl.multiple_of(c * CHUNK + h * HALF, HALF), HALF)]
+        for i in FAR:
+            j = lax.rem(c + i, CH)
+            put(
+                osnd.at[h, pl.ds(pl.multiple_of(j * OWN, OWN), OWN), :],
+                o_dst,
+                s6.at[h],
+                r6.at[h],
+                (s, j),
+            )
+        pltpu.make_async_copy(osnd.at[h, rows_own, :], o_dst, r6.at[h]).start()
+
+    mix(0)
+    mix(1)
+
+    for h in range(2):
+        wait(out_ref.at[:, pl.ds(0, SPAN // 2)], r6.at[h])
     most = pl.ds(0, CH - 1)
     wait(pbuf.at[most, 0], s1.at[0])
-    for part, js, _ in parts:
-
-        @pl.when(pk == part)
-        def _():
-            wait(wbuf.at[js, most, 0, :, pl.ds(0, LANES)], s1.at[1])
-            wait(wbuf.at[js, pl.ds(0, 6)], s1.at[5])
-            wait(wbuf.at[js], s1.at[6])
-
+    wait(wbuf.at[:, most, 0, :, pl.ds(0, LANES)], s1.at[1])
+    wait(wbuf.at[:, pl.ds(0, 6), pl.ds(0, 2)], s1.at[5])
+    wait(wbuf.at[:, :, pl.ds(0, 2)], s1.at[6])
     wait(xc.at[pl.ds(0, D - OWN), pl.ds(HALO, CHUNK)], s1.at[2])
     tails = pl.ds(0, OWN)
     wait(xc.at[pl.ds(0, 6 * OWN), pl.ds(0, HALO)], s1.at[3])
@@ -643,9 +658,10 @@
 
     wait(pbuf.at[pl.ds(0, 6)], s1.at[4])
     wait(ksnd.at[pl.ds(0, SEQ - 1)], s3.at[0])
-    for i, buf in ((1, gsnd), (2, ysnd)):
-        wait(buf.at[pl.ds(0, DEV - 1)], s3.at[i])
-    wait(osnd.at[pl.ds(0, D - OWN), :], s6)
+    wait(gsnd.at[pl.ds(0, DEV - 1)], s3.at[1])
+    for h in range(2):
+        wait(ysnd.at[h, pl.ds(0, DEV - 1)], s3.at[3 + h])
+        wait(osnd.at[h, pl.ds(0, D - OWN), :], s6.at[h])
 
 
 def body(
@@ -689,13 +705,14 @@
             vmem((16, ORDER), F32),
             vmem((OWN, LANES), F32),
             vmem((D, HALO + CHUNK), BF16),
-            vmem((3, CH, 2, 16, D), BF16),
+            vmem((3, CH, 4, 8, D), BF16),
             vmem((CH, 4, 8, LANES), F32),
             vmem((D, LANES), F32),
             vmem((2, D, CHUNK), BF16),
             vmem((9, 2, D, LANES), F32),
             vmem((6, D, LANES), F32),
             vmem((DEV, RADIX, LANES), F32),
+            vmem((DEV, PAIR, LANES), F32),
             vmem((D, CHUNK), F32),
             vmem((D, CHUNK), F32),
             vmem((3, D, D), F32),
@@ -722,18 +739,19 @@
             vmem((RADIX, 2, D, LANES), F32),
             vmem((2 * D, CHUNK), BF16),
             vmem((2 * D, CHUNK), BF16),
-            vmem((DEV, RADIX, LANES), BF16),
-            vmem((DEV, RADIX, LANES), BF16),
-            vmem((D, CHUNK), BF16),
+            vmem((2, DEV, PAIR, LANES), BF16),
+            vmem((2, DEV, PAIR, LANES), BF16),
+            vmem((2, D, HALF), BF16),
             dma((12,)),
             dma((7,)),
+            dma((3,)),
             pltpu.SemaphoreType.REGULAR,
-            dma((7,)),
-            dma((7,)),
-            dma((3,)),
-            dma((3,)),
-            dma,
-            dma,
+            dma((8,)),
+            dma((8,)),
+            dma((5,)),
+            dma((5,)),
+            dma((2,)),
+            dma((2,)),
         ],
         compiler_params=pltpu.CompilerParams(collective_id=0, has_side_effects=True),
     )(

time: 58 us -> 55.2 us (0.952)
  Pallas kernels: 57.2 us -> 54.4 us
    pallas_call x1, Pallas kernels: 57.2 us -> 54.4 us  [body(): pl.pallas_call(kernel, out_shape=pltpu.VMEM((OWN, SPAN), BF16), in_specs=...]
where the time goes in v4:
time: 55.2 us; the launch traced here: 55.1 us
  Pallas kernels  54.4 us (99%)
  local copies, waits for them, and re-layouts  0.71 us (1%)
    pallas_call x1, Pallas kernels, body(): pl.pallas_call(kernel, out_shape=pltpu.VMEM((OWN, SPAN), BF16), in_specs=...  54.4 us

profile of v4, /device:TPU:1, one launch (start us, length us, event | category | flops | bytes accessed | tf_op | source)
XLA Modules:
  0.0 55.1 jit_solution(17455203848551597156)
XLA Ops:
  0.0 54.4 %shard_map.199 = bf16[32,4096]{1,0:T(8,128)(2,1)S(1)} custom-call(bf16[32,4096]{1,0:T(8,128)(2,1)} %x_ref.1, bf16[3,32,256]{2,1,0:T(8,128)(2,1)} %w_ref.1, f32[3,32]{1,0:T(4,128)} %bin_ref.1, f32[3,3,32]{2,1,0:T(4,128)} %bitcast.5, f32[32,64]{1,0:T(8,128)} %fout_ref.1, f32[1,32]{1,0:T(1,128)} %bitcast.7, f32[1,32]{1,0:T(1,128)} %bitcast.8, f32[1,32]{1,0:T(1,128)} %bitcast.9, ...), custom_call_target="tpu_custom_call" | custom-call | tf_op jit(solution)/shard_map/pallas_call | solution.py:686
  54.4 0.7 %copy.23 = bf16[32,4096]{1,0:T(8,128)(2,1)} copy(bf16[32,4096]{1,0:T(8,128)(2,1)S(1)} %shard_map.199) | data formatting | bytes 524288

commit v5 on v4

--- a/solution.py
+++ b/solution.py
@@ -120,6 +120,7 @@
     raw,
     rawnet,
     prm,
+    psend,
     xc,
     wbuf,
     pbuf,
@@ -248,7 +249,12 @@
 
     prm[...] = jnp.zeros_like(prm)
     mine = columns(raw[...], OWN)
-    prm[:, 0:16] = mine
+    left = mine
+    for i in range(3):
+        part = left.astype(BF16)
+        prm[:, 16 * i : 16 * i + 16] = part.astype(F32)
+        left = left - part.astype(F32)
+    psend[...] = prm[...].reshape(4, 8, LANES).astype(BF16)
     pl.semaphore_wait(bar, jnp.where(s < SEQ - 1, SEQ + CH - 1, SEQ + CH - 2))
 
     def put(src, dst, send, recv, to):
@@ -260,11 +266,10 @@
         pltpu.make_async_copy(ref, ref, sem).wait()
 
     half = pl.ds(pl.multiple_of(lax.rem(quad, 2) * LANES, LANES), LANES)
-    quarter = pl.ds(pl.multiple_of(quad * 8, 8), 8)
     octet = 2 * pk + quad // 2
     w_src = w_ref.at[:, pl.ds(pl.multiple_of(octet * 8, 8), 8), half]
     w_dst = wbuf.at[:, c, octet, :, half]
-    p_src = prm.at[quarter, :]
+    p_src = psend.at[quad]
     p_dst = pbuf.at[c, quad]
     x_dst = xc.at[rows_own, pl.ds(HALO, CHUNK)]
     h_dst = xc.at[rows_own, pl.ds(0, HALO)]
@@ -411,17 +416,6 @@
 
     hand_over(1)
     hand_over(3)
-    for copy in consts:
-        copy.wait()
-    for i in range(6):
-        at = 1 + i if i < 3 else 2 + i
-        spins[i] = jnp.broadcast_to(spin_v[:, at : at + 1], (D, LANES))
-    for h in range(RADIX):
-        lanes = slice(h * LANES, (h + 1) * LANES)
-        cs, sn = step_v[h : h + 1, :], step_v[RADIX + h : RADIX + h + 1, :]
-        twid_v[0, :, lanes] = base_v[0] * cs - base_v[1] * sn
-        twid_v[1, :, lanes] = base_v[1] * cs + base_v[0] * sn
-
     spots = [(i, j, l) for i in range(4) for j in range(4) for l in range(2)]
     spots.sort(key=lambda o: -(min(o[0], 4 - o[0]) + min(o[1], 4 - o[1])))
     spots = [o for o in spots if o != (0, 0, 0)] + [(0, 0, 0)]
@@ -431,14 +425,23 @@
 
     hand_over(2)
     wait(pbuf.at[pl.ds(0, 6)], r1.at[4])
-    pflat[...] = pbuf[...].reshape(D, LANES)
+    arrived = pbuf[...].astype(F32).reshape(D, LANES)
+    pflat[...] = arrived + (
+        pltpu.roll(arrived, LANES - 16, 1) + pltpu.roll(arrived, LANES - 32, 1)
+    )
     for j in range(3):
         bias = jnp.broadcast_to(pflat[:, BIAS + j : BIAS + j + 1], (D, LANES))
+        total = None
         for i in range(3):
             at = TAPS + 3 * j + i
             tap = jnp.broadcast_to(pflat[:, at : at + 1], (D, LANES))
-            cols[3 * j + i, 0] = tap
-            cols[3 * j + i, 1] = tap * bias
+            cols[3 * j + i] = tap
+            total = tap * bias if total is None else total + tap * bias
+            if i < 2:
+                cols[9 + 3 * j + i] = tap * bias
+            else:
+                cols[11 + 3 * j] = total
+                cols[18 + j] = tap * bias
 
     pl.semaphore_wait(gate, SEQ - 1)
     wait(xc.at[:, pl.ds(HALO, CHUNK)], r1.at[2])
@@ -464,14 +467,15 @@
             lanes = slice(r * LANES, (r + 1) * LANES)
             streams = []
             for j in range(3):
-                total = None
+                if r:
+                    total = cols[11 + 3 * j, rows, :]
+                else:
+                    total = cols[18 + j, rows, :]
+                    for i in range(2):
+                        total = total + cols[9 + 3 * j + i, rows, :] * started[i]
                 for i in range(3):
-                    shifted_bias = cols[3 * j + i, 1, rows, :]
-                    if r == 0 and i < 2:
-                        shifted_bias = shifted_bias * started[i]
-                    term = cols[3 * j + i, 0, rows, :] * taken[i][64 * j : 64 * j + 64, lanes]
-                    term = term + shifted_bias
-                    total = term if total is None else total + term
+                    part = taken[i][64 * j : 64 * j + 64, lanes]
+                    total = total + cols[3 * j + i, rows, :] * part
                 streams.append(total)
             gated = streams[2] * streams[1]
             keep0[rows, lanes] = streams[0]
@@ -498,6 +502,18 @@
         return carry
 
     lax.fori_loop(0, 4, gates, 0)
+
+    for copy in consts:
+        copy.wait()
+    for i in range(6):
+        at = 1 + i if i < 3 else 2 + i
+        spins[i] = jnp.broadcast_to(spin_v[:, at : at + 1], (D, LANES))
+    for h in range(RADIX):
+        lanes = slice(h * LANES, (h + 1) * LANES)
+        cs, sn = step_v[h : h + 1, :], step_v[RADIX + h : RADIX + h + 1, :]
+        twid_v[0, :, lanes] = base_v[0] * cs - base_v[1] * sn
+        twid_v[1, :, lanes] = base_v[1] * cs + base_v[0] * sn
+
 
     def whole(rcv):
         stage[...] = rcv[...].astype(F32)
@@ -704,12 +720,13 @@
             vmem((16, OWN), F32),
             vmem((16, ORDER), F32),
             vmem((OWN, LANES), F32),
+            vmem((4, 8, LANES), BF16),
             vmem((D, HALO + CHUNK), BF16),
             vmem((3, CH, 4, 8, D), BF16),
-            vmem((CH, 4, 8, LANES), F32),
+            vmem((CH, 4, 8, LANES), BF16),
             vmem((D, LANES), F32),
             vmem((2, D, CHUNK), BF16),
-            vmem((9, 2, D, LANES), F32),
+            vmem((21, D, LANES), F32),
             vmem((6, D, LANES), F32),
             vmem((DEV, RADIX, LANES), F32),
             vmem((DEV, PAIR, LANES), F32),

time: 55.2 us -> 53.2 us (0.964)
  Pallas kernels: 54.4 us -> 52.4 us
    pallas_call x1, Pallas kernels: 54.4 us -> 52.4 us  [body(): pl.pallas_call(kernel, out_shape=pltpu.VMEM((OWN, SPAN), BF16), in_specs=...]
where the time goes in v5:
time: 53.2 us; the launch traced here: 53.1 us
  Pallas kernels  52.4 us (98%)
  local copies, waits for them, and re-layouts  0.71 us (1%)
    pallas_call x1, Pallas kernels, body(): pl.pallas_call(kernel, out_shape=pltpu.VMEM((OWN, SPAN), BF16), in_specs=...  52.4 us

profile of v5, /device:TPU:1, one launch (start us, length us, event | category | flops | bytes accessed | tf_op | source)
XLA Modules:
  0.0 53.1 jit_solution(6530555706226985498)
XLA Ops:
  0.0 52.4 %shard_map.199 = bf16[32,4096]{1,0:T(8,128)(2,1)S(1)} custom-call(bf16[32,4096]{1,0:T(8,128)(2,1)} %x_ref.1, bf16[3,32,256]{2,1,0:T(8,128)(2,1)} %w_ref.1, f32[3,32]{1,0:T(4,128)} %bin_ref.1, f32[3,3,32]{2,1,0:T(4,128)} %bitcast.5, f32[32,64]{1,0:T(8,128)} %fout_ref.1, f32[1,32]{1,0:T(1,128)} %bitcast.7, f32[1,32]{1,0:T(1,128)} %bitcast.8, f32[1,32]{1,0:T(1,128)} %bitcast.9, ...), custom_call_target="tpu_custom_call" | custom-call | tf_op jit(solution)/shard_map/pallas_call | solution.py:702
  52.4 0.7 %copy.23 = bf16[32,4096]{1,0:T(8,128)(2,1)} copy(bf16[32,4096]{1,0:T(8,128)(2,1)S(1)} %shard_map.199) | data formatting | bytes 524288

commit v6 on v5

--- a/solution.py
+++ b/solution.py
@@ -121,6 +121,10 @@
     rawnet,
     prm,
     psend,
+    ends,
+    tails,
+    halo,
+    before,
     xc,
     wbuf,
     pbuf,
@@ -160,6 +164,7 @@
     yrcv,
     osnd,
     small_sem,
+    end_sem,
     const_sem,
     ring_sem,
     gate,
@@ -213,6 +218,10 @@
     ]
     for copy in smalls:
         copy.start()
+    for j in range(CH):
+        pltpu.make_async_copy(
+            x_ref.at[:, pl.ds((j + 1) * CHUNK - HALO, HALO)], ends.at[j], end_sem
+        ).start()
 
     bar = pltpu.get_barrier_semaphore()
 
@@ -255,68 +264,19 @@
         prm[:, 16 * i : 16 * i + 16] = part.astype(F32)
         left = left - part.astype(F32)
     psend[...] = prm[...].reshape(4, 8, LANES).astype(BF16)
-    pl.semaphore_wait(bar, jnp.where(s < SEQ - 1, SEQ + CH - 1, SEQ + CH - 2))
-
-    def put(src, dst, send, recv, to):
-        pltpu.make_async_remote_copy(
-            src_ref=src, dst_ref=dst, send_sem=send, recv_sem=recv, device_id=to, device_id_type=MESH
-        ).start()
-
-    def wait(ref, sem):
-        pltpu.make_async_copy(ref, ref, sem).wait()
-
-    half = pl.ds(pl.multiple_of(lax.rem(quad, 2) * LANES, LANES), LANES)
-    octet = 2 * pk + quad // 2
-    w_src = w_ref.at[:, pl.ds(pl.multiple_of(octet * 8, 8), 8), half]
-    w_dst = wbuf.at[:, c, octet, :, half]
-    p_src = psend.at[quad]
-    p_dst = pbuf.at[c, quad]
-    x_dst = xc.at[rows_own, pl.ds(HALO, CHUNK)]
-    h_dst = xc.at[rows_own, pl.ds(0, HALO)]
-
-    def chunk(j):
-        return x_ref.at[:, pl.ds(pl.multiple_of(j * CHUNK, CHUNK), CHUNK)]
-
-    def tail(j):
-        return x_ref.at[:, pl.ds(pl.multiple_of(j * CHUNK + CHUNK - HALO, HALO), HALO)]
-
-    for i in FAR:
-        put(p_src, p_dst, s1.at[0], r1.at[0], (s, lax.rem(c + i, CH)))
-    for i in FAR:
-        put(w_src, w_dst, s1.at[1], r1.at[1], (s, lax.rem(c + i, CH)))
-
-    @pl.when(s < SEQ - 1)
-    def _():
-        put(tail(CH - 1), h_dst, s1.at[3], r1.at[3], (s + 1, 0))
-
-    for i in FAR:
-        j = lax.rem(c + i, CH)
-        put(chunk(j), x_dst, s1.at[2], r1.at[2], (s, j))
-
-        @pl.when(j > 0)
-        def _():
-            put(tail(j - 1), h_dst, s1.at[3], r1.at[3], (s, j))
-
-
-    pltpu.make_async_copy(p_src, p_dst, r1.at[0]).start()
-    pltpu.make_async_copy(w_src, w_dst, r1.at[1]).start()
-    pltpu.make_async_copy(chunk(c), x_dst, r1.at[2]).start()
-
-    @pl.when(c > 0)
-    def _():
-        pltpu.make_async_copy(tail(c - 1), h_dst, r1.at[3]).start()
-
-    @pl.when(me == 0)
-    def _():
-        xc[:, 0:HALO] = jnp.zeros((D, HALO), BF16)
-
-    for i in range(1, SEQ):
-        greet(gate, (lax.rem(s + i, SEQ), c))
-    for copy in consts:
-        copy.start()
-    for i in (2, 6, 7, 8, 9, 10, 11):
+    pick = (
+        lax.broadcasted_iota(jnp.int32, (8, HALO), 1)
+        == lax.broadcasted_iota(jnp.int32, (8, HALO), 0) + HALO - 2
+    ).astype(BF16)
+    tails[...] = jnp.zeros_like(tails)
+    pltpu.make_async_copy(ends, ends, end_sem).wait()
+    for j in range(CH):
+        turned_end = lax.dot_general(
+            pick, ends[j], (((1,), (1,)), ((), ())), preferred_element_type=F32
+        )
+        tails[j, :, 0:OWN] = turned_end.astype(BF16)
+    for i in (2, 7, 8, 9, 10):
         smalls[i].wait()
-
     rawnet[...] = jnp.zeros_like(rawnet)
     rawnet[0:5, :] = fin_v[...]
     rawnet[5:8, :] = fbias_v[...]
@@ -332,6 +292,61 @@
         high, low = split(diag[i])
         weight[i, 0:D] = high
         weight[i, D : 2 * D] = low
+
+    pl.semaphore_wait(bar, jnp.where(s < SEQ - 1, SEQ + CH - 1, SEQ + CH - 2))
+
+    def put(src, dst, send, recv, to):
+        pltpu.make_async_remote_copy(
+            src_ref=src, dst_ref=dst, send_sem=send, recv_sem=recv, device_id=to, device_id_type=MESH
+        ).start()
+
+    def wait(ref, sem):
+        pltpu.make_async_copy(ref, ref, sem).wait()
+
+    half = pl.ds(pl.multiple_of(lax.rem(quad, 2) * LANES, LANES), LANES)
+    octet = 2 * pk + quad // 2
+    w_src = w_ref.at[:, pl.ds(pl.multiple_of(octet * 8, 8), 8), half]
+    w_dst = wbuf.at[:, c, octet, :, half]
+    p_src = psend.at[quad]
+    p_dst = pbuf.at[c, quad]
+    x_dst = xc.at[rows_own, :]
+    h_dst = halo.at[c]
+
+    def chunk(j):
+        return x_ref.at[:, pl.ds(pl.multiple_of(j * CHUNK, CHUNK), CHUNK)]
+
+    for i in FAR:
+        put(p_src, p_dst, s1.at[0], r1.at[0], (s, lax.rem(c + i, CH)))
+    for i in FAR:
+        put(w_src, w_dst, s1.at[1], r1.at[1], (s, lax.rem(c + i, CH)))
+
+    @pl.when(s < SEQ - 1)
+    def _():
+        put(tails.at[CH - 1], h_dst, s1.at[3], r1.at[3], (s + 1, 0))
+
+    for i in FAR:
+        j = lax.rem(c + i, CH)
+        put(chunk(j), x_dst, s1.at[2], r1.at[2], (s, j))
+
+        @pl.when(j > 0)
+        def _():
+            put(tails.at[j - 1], h_dst, s1.at[3], r1.at[3], (s, j))
+
+
+    pltpu.make_async_copy(p_src, p_dst, r1.at[0]).start()
+    pltpu.make_async_copy(w_src, w_dst, r1.at[1]).start()
+    pltpu.make_async_copy(chunk(c), x_dst, r1.at[2]).start()
+
+    @pl.when(c > 0)
+    def _():
+        pltpu.make_async_copy(tails.at[c - 1], h_dst, r1.at[3]).start()
+
+    for i in range(1, SEQ):
+        greet(gate, (lax.rem(s + i, SEQ), c))
+    for copy in consts:
+        copy.start()
+    for i in (6, 11):
+        smalls[i].wait()
 
     def tile(step):
         b, side = step // 2, lax.rem(step, 2)
@@ -443,16 +458,27 @@
                 cols[11 + 3 * j] = total
                 cols[18 + j] = tap * bias
 
-    pl.semaphore_wait(gate, SEQ - 1)
-    wait(xc.at[:, pl.ds(HALO, CHUNK)], r1.at[2])
+    before[...] = jnp.zeros_like(before)
 
     @pl.when(me > 0)
     def _():
-        wait(xc.at[:, pl.ds(0, HALO)], r1.at[3])
+        wait(halo, r1.at[3])
+        eye = (
+            lax.broadcasted_iota(jnp.int32, (OWN, OWN), 0)
+            == lax.broadcasted_iota(jnp.int32, (OWN, OWN), 1)
+        ).astype(BF16)
+        for j in range(CH):
+            pair_columns = lax.dot_general(
+                eye, halo[j, :, 0:OWN], (((1,), (1,)), ((), ())), preferred_element_type=F32
+            )
+            before[j * OWN : (j + 1) * OWN, HALO - 2 : HALO] = pair_columns[:, 0:2]
+
+    pl.semaphore_wait(gate, SEQ - 1)
+    wait(xc, r1.at[2])
 
     wait(wbuf.at[:, :, pl.ds(0, 2)], r1.at[6])
 
-    wide = xc[...].astype(F32)
+    wide = jnp.concatenate([before[...], xc[...].astype(F32)], axis=1)
     for i in (0, 1):
         xs[i] = pltpu.roll(wide, 2 - i, 1)[:, HALO:].astype(BF16)
     place = lax.broadcasted_iota(jnp.int32, (1, LANES), 1)
@@ -462,7 +488,7 @@
         pair = lax.rem(c // 2 + 2 + (t + 1) // 2 * (1 - 2 * lax.rem(t, 2)), 4)
         rows = pl.ds(pl.multiple_of(pair * 64, 64), 64)
         w = wbuf[:, pl.ds(pair * 2, 2)].astype(F32).reshape(3 * 64, D).astype(BF16)
-        taken = [mm(w, xs[0]), mm(w, xs[1]), mm(w, xc[:, HALO:])]
+        taken = [mm(w, xs[0]), mm(w, xs[1]), mm(w, xc[...])]
         for r in range(RADIX):
             lanes = slice(r * LANES, (r + 1) * LANES)
             streams = []
@@ -660,17 +686,16 @@
     wait(wbuf.at[:, most, 0, :, pl.ds(0, LANES)], s1.at[1])
     wait(wbuf.at[:, pl.ds(0, 6), pl.ds(0, 2)], s1.at[5])
     wait(wbuf.at[:, :, pl.ds(0, 2)], s1.at[6])
-    wait(xc.at[pl.ds(0, D - OWN), pl.ds(HALO, CHUNK)], s1.at[2])
-    tails = pl.ds(0, OWN)
-    wait(xc.at[pl.ds(0, 6 * OWN), pl.ds(0, HALO)], s1.at[3])
+    wait(xc.at[pl.ds(0, D - OWN), :], s1.at[2])
+    wait(halo.at[pl.ds(0, 6)], s1.at[3])
 
     @pl.when(c == 0)
     def _():
-        wait(xc.at[tails, pl.ds(0, HALO)], s1.at[3])
+        wait(halo.at[0], s1.at[3])
 
     @pl.when(s < SEQ - 1)
     def _():
-        wait(xc.at[tails, pl.ds(0, HALO)], s1.at[3])
+        wait(halo.at[0], s1.at[3])
 
     wait(pbuf.at[pl.ds(0, 6)], s1.at[4])
     wait(ksnd.at[pl.ds(0, SEQ - 1)], s3.at[0])
@@ -721,7 +746,11 @@
             vmem((16, ORDER), F32),
             vmem((OWN, LANES), F32),
             vmem((4, 8, LANES), BF16),
-            vmem((D, HALO + CHUNK), BF16),
+            vmem((CH, OWN, HALO), BF16),
+            vmem((CH, 8, LANES), BF16),
+            vmem((CH, 8, LANES), BF16),
+            vmem((D, HALO), F32),
+            vmem((D, CHUNK), BF16),
             vmem((3, CH, 4, 8, D), BF16),
             vmem((CH, 4, 8, LANES), BF16),
             vmem((D, LANES), F32),
@@ -760,6 +789,7 @@
             vmem((2, DEV, PAIR, LANES), BF16),
             vmem((2, D, HALF), BF16),
             dma((12,)),
+            dma,
             dma((7,)),
             dma((3,)),
             pltpu.SemaphoreType.REGULAR,

time: 53.2 us -> 53.2 us (level)
  no operation moved by 1% of the time
where the time goes in v6:
time: 53.2 us; the launch traced here: 53.1 us
  Pallas kernels  52.4 us (98%)
  local copies, waits for them, and re-layouts  0.71 us (1%)
    pallas_call x1, Pallas kernels, body(): pl.pallas_call(kernel, out_shape=pltpu.VMEM((OWN, SPAN), BF16), in_specs=...  52.4 us

profile of v6, /device:TPU:1, one launch (start us, length us, event | category | flops | bytes accessed | tf_op | source)
XLA Modules:
  0.0 53.1 jit_solution(6836592705569129866)
XLA Ops:
  0.0 52.4 %shard_map.199 = bf16[32,4096]{1,0:T(8,128)(2,1)S(1)} custom-call(bf16[32,4096]{1,0:T(8,128)(2,1)} %x_ref.1, bf16[3,32,256]{2,1,0:T(8,128)(2,1)} %w_ref.1, f32[3,32]{1,0:T(4,128)} %bin_ref.1, f32[3,3,32]{2,1,0:T(4,128)} %bitcast.5, f32[32,64]{1,0:T(8,128)} %fout_ref.1, f32[1,32]{1,0:T(1,128)} %bitcast.7, f32[1,32]{1,0:T(1,128)} %bitcast.8, f32[1,32]{1,0:T(1,128)} %bitcast.9, ...), custom_call_target="tpu_custom_call" | custom-call | tf_op jit(solution)/shard_map/pallas_call | solution.py:727
  52.4 0.7 %copy.23 = bf16[32,4096]{1,0:T(8,128)(2,1)} copy(bf16[32,4096]{1,0:T(8,128)(2,1)S(1)} %shard_map.199) | data formatting | bytes 524288

commit v7 on v5

--- a/solution.py
+++ b/solution.py
@@ -255,68 +255,8 @@
         prm[:, 16 * i : 16 * i + 16] = part.astype(F32)
         left = left - part.astype(F32)
     psend[...] = prm[...].reshape(4, 8, LANES).astype(BF16)
-    pl.semaphore_wait(bar, jnp.where(s < SEQ - 1, SEQ + CH - 1, SEQ + CH - 2))
-
-    def put(src, dst, send, recv, to):
-        pltpu.make_async_remote_copy(
-            src_ref=src, dst_ref=dst, send_sem=send, recv_sem=recv, device_id=to, device_id_type=MESH
-        ).start()
-
-    def wait(ref, sem):
-        pltpu.make_async_copy(ref, ref, sem).wait()
-
-    half = pl.ds(pl.multiple_of(lax.rem(quad, 2) * LANES, LANES), LANES)
-    octet = 2 * pk + quad // 2
-    w_src = w_ref.at[:, pl.ds(pl.multiple_of(octet * 8, 8), 8), half]
-    w_dst = wbuf.at[:, c, octet, :, half]
-    p_src = psend.at[quad]
-    p_dst = pbuf.at[c, quad]
-    x_dst = xc.at[rows_own, pl.ds(HALO, CHUNK)]
-    h_dst = xc.at[rows_own, pl.ds(0, HALO)]
-
-    def chunk(j):
-        return x_ref.at[:, pl.ds(pl.multiple_of(j * CHUNK, CHUNK), CHUNK)]
-
-    def tail(j):
-        return x_ref.at[:, pl.ds(pl.multiple_of(j * CHUNK + CHUNK - HALO, HALO), HALO)]
-
-    for i in FAR:
-        put(p_src, p_dst, s1.at[0], r1.at[0], (s, lax.rem(c + i, CH)))
-    for i in FAR:
-        put(w_src, w_dst, s1.at[1], r1.at[1], (s, lax.rem(c + i, CH)))
-
-    @pl.when(s < SEQ - 1)
-    def _():
-        put(tail(CH - 1), h_dst, s1.at[3], r1.at[3], (s + 1, 0))
-
-    for i in FAR:
-        j = lax.rem(c + i, CH)
-        put(chunk(j), x_dst, s1.at[2], r1.at[2], (s, j))
-
-        @pl.when(j > 0)
-        def _():
-            put(tail(j - 1), h_dst, s1.at[3], r1.at[3], (s, j))
-
-
-    pltpu.make_async_copy(p_src, p_dst, r1.at[0]).start()
-    pltpu.make_async_copy(w_src, w_dst, r1.at[1]).start()
-    pltpu.make_async_copy(chunk(c), x_dst, r1.at[2]).start()
-
-    @pl.when(c > 0)
-    def _():
-        pltpu.make_async_copy(tail(c - 1), h_dst, r1.at[3]).start()
-
-    @pl.when(me == 0)
-    def _():
-        xc[:, 0:HALO] = jnp.zeros((D, HALO), BF16)
-
-    for i in range(1, SEQ):
-        greet(gate, (lax.rem(s + i, SEQ), c))
-    for copy in consts:
-        copy.start()
-    for i in (2, 6, 7, 8, 9, 10, 11):
+    for i in (2, 7, 8, 9, 10):
         smalls[i].wait()
-
     rawnet[...] = jnp.zeros_like(rawnet)
     rawnet[0:5, :] = fin_v[...]
     rawnet[5:8, :] = fbias_v[...]
@@ -332,6 +272,68 @@
         high, low = split(diag[i])
         weight[i, 0:D] = high
         weight[i, D : 2 * D] = low
+
+    pl.semaphore_wait(bar, jnp.where(s < SEQ - 1, SEQ + CH - 1, SEQ + CH - 2))
+
+    def put(src, dst, send, recv, to):
+        pltpu.make_async_remote_copy(
+            src_ref=src, dst_ref=dst, send_sem=send, recv_sem=recv, device_id=to, device_id_type=MESH
+        ).start()
+
+    def wait(ref, sem):
+        pltpu.make_async_copy(ref, ref, sem).wait()
+
+    half = pl.ds(pl.multiple_of(lax.rem(quad, 2) * LANES, LANES), LANES)
+    octet = 2 * pk + quad // 2
+    w_src = w_ref.at[:, pl.ds(pl.multiple_of(octet * 8, 8), 8), half]
+    w_dst = wbuf.at[:, c, octet, :, half]
+    p_src = psend.at[quad]
+    p_dst = pbuf.at[c, quad]
+    x_dst = xc.at[rows_own, pl.ds(HALO, CHUNK)]
+    h_dst = xc.at[rows_own, pl.ds(0, HALO)]
+
+    def chunk(j):
+        return x_ref.at[:, pl.ds(pl.multiple_of(j * CHUNK, CHUNK), CHUNK)]
+
+    def tail(j):
+        return x_ref.at[:, pl.ds(pl.multiple_of(j * CHUNK + CHUNK - HALO, HALO), HALO)]
+
+    for i in FAR:
+        put(p_src, p_dst, s1.at[0], r1.at[0], (s, lax.rem(c + i, CH)))
+    for i in FAR:
+        put(w_src, w_dst, s1.at[1], r1.at[1], (s, lax.rem(c + i, CH)))
+
+    @pl.when(s < SEQ - 1)
+    def _():
+        put(tail(CH - 1), h_dst, s1.at[3], r1.at[3], (s + 1, 0))
+
+    for i in FAR:
+        j = lax.rem(c + i, CH)
+        put(chunk(j), x_dst, s1.at[2], r1.at[2], (s, j))
+
+        @pl.when(j > 0)
+        def _():
+            put(tail(j - 1), h_dst, s1.at[3], r1.at[3], (s, j))
+
+
+    pltpu.make_async_copy(p_src, p_dst, r1.at[0]).start()
+    pltpu.make_async_copy(w_src, w_dst, r1.at[1]).start()
+    pltpu.make_async_copy(chunk(c), x_dst, r1.at[2]).start()
+
+    @pl.when(c > 0)
+    def _():
+        pltpu.make_async_copy(tail(c - 1), h_dst, r1.at[3]).start()
+
+    @pl.when(me == 0)
+    def _():
+        xc[:, 0:HALO] = jnp.zeros((D, HALO), BF16)
+
+    for i in range(1, SEQ):
+        greet(gate, (lax.rem(s + i, SEQ), c))
+    for copy in consts:
+        copy.start()
+    for i in (6, 11):
+        smalls[i].wait()
 
     def tile(step):
         b, side = step // 2, lax.rem(step, 2)

time: 53.2 us -> 53 us (level)
  no operation moved by 1% of the time
where the time goes in v7:
time: 53 us; the launch traced here: 52.9 us
  Pallas kernels  52.2 us (98%)
  local copies, waits for them, and re-layouts  0.71 us (1%)
    pallas_call x1, Pallas kernels, body(): pl.pallas_call(kernel, out_shape=pltpu.VMEM((OWN, SPAN), BF16), in_specs=...  52.2 us

profile of v7, /device:TPU:1, one launch (start us, length us, event | category | flops | bytes accessed | tf_op | source)
XLA Modules:
  0.0 52.9 jit_solution(11831349855135489916)
XLA Ops:
  0.0 52.2 %shard_map.199 = bf16[32,4096]{1,0:T(8,128)(2,1)S(1)} custom-call(bf16[32,4096]{1,0:T(8,128)(2,1)} %x_ref.1, bf16[3,32,256]{2,1,0:T(8,128)(2,1)} %w_ref.1, f32[3,32]{1,0:T(4,128)} %bin_ref.1, f32[3,3,32]{2,1,0:T(4,128)} %bitcast.5, f32[32,64]{1,0:T(8,128)} %fout_ref.1, f32[1,32]{1,0:T(1,128)} %bitcast.7, f32[1,32]{1,0:T(1,128)} %bitcast.8, f32[1,32]{1,0:T(1,128)} %bitcast.9, ...), custom_call_target="tpu_custom_call" | custom-call | tf_op jit(solution)/shard_map/pallas_call | solution.py:704
  52.2 0.7 %copy.23 = bf16[32,4096]{1,0:T(8,128)(2,1)} copy(bf16[32,4096]{1,0:T(8,128)(2,1)S(1)} %shard_map.199) | data formatting | bytes 524288
